TPU v7x, 32 devices: a whole 2x2x4 slice. The times are simulated.
32 devices in a mesh: row: 8 (over y, x, core), col: 4 (over z).
Axes of the slice: x: 2, y: 2, z: 4, core: 2. Of those that a mesh axis runs over, the one named last changes fastest.
Arguments:
- matrix: float32 [16, 1024, 32, 512], P(None, 'row', None, 'col'), may hold values from -21 to 21
Outputs:
- reduced: float32 [16, 1024, 32, 512], P(None, 'row', None, 'col')
- reflectors: float32 [16, 1024, 256], P(None, 'row')
All inputs are finite; a program needn't handle non-finite values.
Results may differ from a plain program's by a relative error of at most 0.00011.
Values sent between devices are 32-bit elements; how exact they have to be, the bound alone decides.
A program may use at most 320 MiB of HBM per device.

v0:
```python
import functools

import jax
import jax.numpy as jnp
from jax import lax
from jax.experimental import pallas as pl
from jax.experimental.pallas import tpu as pltpu
from jax.sharding import PartitionSpec as P

PANELS = 2
MESH = pl.DeviceIdType.MESH
VMEM_LIMIT = 60 * 1024 * 1024


def dot_highest(left, right):
    return jnp.dot(left, right, precision=lax.Precision.HIGHEST, preferred_element_type=jnp.float32)


def greet(*axes):
    barrier = pltpu.get_barrier_semaphore()
    total = 0
    for axis in axes:
        me, size = lax.axis_index(axis), lax.axis_size(axis)
        for step in range(1, size):
            pl.semaphore_signal(
                barrier, inc=1, device_id={axis: lax.rem(me + step, size)}, device_id_type=MESH
            )
        total += size - 1
    pl.semaphore_wait(barrier, total)


def remote(src, dst, send_sem, recv_sem, **device):
    return pltpu.make_async_remote_copy(
        src_ref=src,
        dst_ref=dst,
        send_sem=send_sem,
        recv_sem=recv_sem,
        device_id=device,
        device_id_type=MESH,
    )


def remote_params(collective_id):
    return pltpu.CompilerParams(
        collective_id=collective_id, has_side_effects=True, vmem_limit_bytes=VMEM_LIMIT
    )

STREAM_CHUNKS = 8

LAG = 2


def ring_place(pair, pairs):
    return pair + (pair // 2) * (1 - 2 * (pair % 2)) if pairs == 4 else pair


class Strip:
    def __init__(self, root, strip_ref, out_ref, ring_send, pair_send, recv, local_sem):
        size = lax.axis_size("row")
        me = lax.axis_index("row")
        pairs = size // 2
        pair, core = me // 2, me % 2
        place = ring_place(pair, pairs)
        distance = (place - ring_place(root // 2, pairs) + pairs) % pairs
        stream = (core + root % 2) % 2
        hop = (distance * (1 - 2 * stream) + stream * pairs) % pairs
        self.target = 2 * ring_place((place + 1 - 2 * stream + pairs) % pairs, pairs) + core
        self.sibling = 2 * pair + 1 - core
        self.root, self.me, self.pairs = root, me, pairs
        self.stream, self.hop, self.distance = stream, hop, distance
        self.strip_ref, self.out_ref = strip_ref, out_ref
        self.ring_send, self.pair_send = ring_send, pair_send
        self.recv, self.local_sem = recv, local_sem
        self.piece = out_ref.shape[0] // (2 * STREAM_CHUNKS)

    def rows_of(self, which, i):
        start = (which * STREAM_CHUNKS + i) * self.piece
        return pl.ds(pl.multiple_of(start, self.piece), self.piece)

    def to_ring(self, i, source, which):
        rows = self.rows_of(which, i)
        return remote(
            source.at[rows],
            self.out_ref.at[rows],
            self.ring_send.at[i],
            self.recv.at[which, i],
            row=self.target,
        )

    def to_sibling(self, i, source, which, slot):
        rows = self.rows_of(which, i)
        return remote(
            source.at[rows],
            self.out_ref.at[rows],
            self.pair_send.at[slot, i],
            self.recv.at[which, i],
            row=self.sibling,
        )

    def root_copies(self):
        copies = []
        for i in range(STREAM_CHUNKS):
            copies.append(self.to_ring(i, self.strip_ref, 0))
            copies.append(self.to_sibling(i, self.strip_ref, 1, 1))
        for i in range(STREAM_CHUNKS):
            copies.append(self.to_sibling(i, self.strip_ref, 0, 0))
        return copies

    def begin(self):
        @pl.when(self.me == self.root)
        def _():
            for copy in self.root_copies():
                copy.start()
            pltpu.make_async_copy(self.strip_ref, self.out_ref, self.local_sem).start()

    def serve(self, i):
        onward = self.to_ring(i, self.out_ref, self.stream)
        onward.wait_recv()

        @pl.when(self.hop < self.pairs - 1)
        def _():
            onward.start()

        @pl.when(self.distance > 0)
        def _():
            self.to_sibling(i, self.out_ref, self.stream, 0).start()

    def serve_turn(self, turn):
        first = 2 * (turn - 2 * self.hop)
        for half in range(2):
            i = first + half

            @pl.when((self.me != self.root) & (i >= 0) & (i < STREAM_CHUNKS))
            def _():
                self.serve(i)

    def turns(self):
        return STREAM_CHUNKS // 2 + 2 * (self.pairs - 1)

    def end(self):
        @pl.when(self.me == self.root)
        def _():
            for copy in self.root_copies():
                copy.wait_send()
            pltpu.make_async_copy(self.strip_ref, self.out_ref, self.local_sem).wait()

        @pl.when(self.me != self.root)
        def _():
            for i in range(STREAM_CHUNKS):
                self.to_ring(i, self.out_ref, 1 - self.stream).wait_recv()

                @pl.when(self.hop < self.pairs - 1)
                def _():
                    self.to_ring(i, self.out_ref, self.stream).wait_send()

                @pl.when(self.distance > 0)
                def _():
                    self.to_sibling(i, self.out_ref, self.stream, 0).wait_send()


STRIP_SEMS = [
    pltpu.SemaphoreType.DMA((STREAM_CHUNKS,)),
    pltpu.SemaphoreType.DMA((2, STREAM_CHUNKS)),
    pltpu.SemaphoreType.DMA((2, STREAM_CHUNKS)),
    pltpu.SemaphoreType.DMA,
]


def strip_kernel(root, layer, a_ref, out_ref, *sems):
    greet("row")
    strip = Strip(root, a_ref.at[layer], out_ref, *sems)
    strip.begin()

    @pl.when(strip.me != root)
    def _():
        for i in range(STREAM_CHUNKS):
            strip.serve(i)

    strip.end()


def spread_strip(matrix, root, layer, collective_id):
    return pl.pallas_call(
        functools.partial(strip_kernel, root, layer),
        out_shape=jax.ShapeDtypeStruct(matrix.shape[1:], matrix.dtype),
        in_specs=[pl.BlockSpec(memory_space=pl.ANY)],
        out_specs=pl.BlockSpec(memory_space=pltpu.VMEM),
        scratch_shapes=STRIP_SEMS,
        compiler_params=remote_params(collective_id),
    )(matrix)


def total_kernel(x_ref, out_ref, held, col_send, col_recv, row_send, row_recv, local_sem):
    rows, cols = lax.axis_size("row"), lax.axis_size("col")
    row, col = lax.axis_index("row"), lax.axis_index("col")
    greet("row", "col")
    own = pltpu.make_async_copy(x_ref.at[row], held.at[col], local_sem)
    own.start()
    copies = []
    for step in range(1, cols):
        copy = remote(
            x_ref.at[row],
            held.at[col],
            col_send.at[step],
            col_recv.at[step],
            col=lax.rem(col + step, cols),
        )
        copy.start()
        copies.append(copy)
    own.wait()
    for copy in copies:
        copy.wait()
    value = held[0]
    for q in range(1, cols):
        value = value + held[q]
    out_ref[row] = value
    copies = []
    for step in range(1, rows):
        copy = remote(
            out_ref.at[row],
            out_ref.at[row],
            row_send.at[step],
            row_recv.at[step],
            row=lax.rem(row + step, rows),
        )
        copy.start()
        copies.append(copy)
    for copy in copies:
        copy.wait()


def total(x, collective_id):
    rows, cols = lax.axis_size("row"), lax.axis_size("col")
    piece = x.shape[0] // rows
    shape = (rows, piece, x.shape[1])
    out = pl.pallas_call(
        total_kernel,
        out_shape=jax.ShapeDtypeStruct(shape, x.dtype),
        in_specs=[pl.BlockSpec(memory_space=pltpu.VMEM)],
        out_specs=pl.BlockSpec(memory_space=pltpu.VMEM),
        scratch_shapes=[
            pltpu.VMEM((cols, piece, x.shape[1]), x.dtype),
            pltpu.SemaphoreType.DMA((cols,)),
            pltpu.SemaphoreType.DMA((cols,)),
            pltpu.SemaphoreType.DMA((rows,)),
            pltpu.SemaphoreType.DMA((rows,)),
            pltpu.SemaphoreType.DMA,
        ],
        compiler_params=remote_params(collective_id),
    )(x.reshape(shape))
    return out.reshape(x.shape)


LEAF = 16


def eliminate(ref, symmetric):
    size = ref.shape[0]
    strip_row = lax.broadcasted_iota(jnp.int32, (LEAF, size), 0)
    strip_lane = lax.broadcasted_iota(jnp.int32, (LEAF, size), 1)
    row = lax.broadcasted_iota(jnp.int32, (size, size), 0)
    lane = lax.broadcasted_iota(jnp.int32, (size, size), 1)

    def block(b, carry):
        start = pl.multiple_of(b * LEAF, LEAF)
        whole = ref[...]
        strip = ref[pl.ds(start, LEAF), :]
        columns = [jnp.broadcast_to(strip[:, i : i + 1], (LEAF, size)) for i in range(LEAF)]
        panel = jnp.where(strip_lane < LEAF, (strip_row == strip_lane).astype(jnp.float32), strip)
        for i in range(LEAF):
            column = columns[i]
            pivot = jnp.broadcast_to(column[i : i + 1, :], (LEAF, size))
            if symmetric:
                scale = lax.rsqrt(pivot)
                scale = scale * (1.5 - 0.5 * pivot * scale * scale)
                column = column * scale
                touched = strip_row > i
            else:
                scale = 1.0 / pivot
                touched = strip_row != i

            def step(x):
                lead = jnp.broadcast_to(x[i : i + 1, :], (LEAF, size)) * scale
                return jnp.where(touched, x - column * lead, jnp.where(strip_row == i, lead, x))

            panel = step(panel)
            for j in range(i + 1, LEAF):
                columns[j] = step(columns[j])
        base = jnp.where(lane < LEAF, 0.0, whole)
        if symmetric:
            factor = jnp.where((strip_lane >= LEAF) & (strip_lane < size - start), panel, 0.0)
            factor = pltpu.roll(factor, start, axis=1)
            change = lax.dot_general(
                factor,
                panel,
                (((0,), (0,)), ((), ())),
                precision=lax.Precision.HIGHEST,
                preferred_element_type=jnp.float32,
            )
            ref[...] = jnp.where(row < start, whole, base - change)
        else:
            inside = (row >= start) & (row < start + LEAF)
            factor = jnp.where(inside | (lane >= LEAF), 0.0, whole)
            padded = jnp.concatenate([panel, jnp.zeros((size - LEAF, size), jnp.float32)], axis=0)
            ref[...] = base - dot_highest(factor, padded)
        ref[pl.ds(start, LEAF), :] = panel
        ref[...] = pltpu.roll(ref[...], size - LEAF, axis=1)
        return carry

    lax.fori_loop(0, size // LEAF, block, 0)
    if symmetric:
        ref[...] = jnp.where(row >= lane, ref[...], 0.0)


def transposed_dot(left, right):
    return lax.dot_general(
        left,
        right,
        (((1,), (1,)), ((), ())),
        precision=lax.Precision.HIGHEST,
        preferred_element_type=jnp.float32,
    )


def factor_kernel(both_ref, lower_ref, top_ref):
    width = both_ref.shape[1]
    lower_ref[...] = both_ref[:width]
    eliminate(lower_ref, True)
    row = lax.broadcasted_iota(jnp.int32, (width, width), 0)
    lane = lax.broadcasted_iota(jnp.int32, (width, width), 1)
    identity = (row == lane).astype(jnp.float32)
    top_ref[...] = transposed_dot(both_ref[width:], lower_ref[...]) - identity


def factorize(both):
    width = both.shape[1]
    return pl.pallas_call(
        factor_kernel,
        out_shape=[jax.ShapeDtypeStruct((width, width), jnp.float32)] * 2,
        compiler_params=pltpu.CompilerParams(vmem_limit_bytes=VMEM_LIMIT),
    )(both)


def split(value):
    high = value.astype(jnp.bfloat16)
    return high, (value - high.astype(jnp.float32)).astype(jnp.bfloat16)


def split_outside(value):
    high = lax.reduce_precision(value, exponent_bits=8, mantissa_bits=7)
    return high.astype(jnp.bfloat16), (value - high).astype(jnp.bfloat16)


def dot_f32(left, right):
    return jnp.dot(left, right, preferred_element_type=jnp.float32)


def tile_copies(a_ref, held, sems, tile, index, slot):
    return [
        pltpu.make_async_copy(
            a_ref.at[pl.ds(index * tile, tile), c, :], held.at[slot, c], sems.at[slot, c]
        )
        for c in range(a_ref.shape[1])
    ]


def fetch_tiles(a_ref, held, sems, tile):
    step, steps = pl.program_id(0), pl.num_programs(0)
    slot = lax.rem(step, 2)

    @pl.when(step == 0)
    def _():
        for copy in tile_copies(a_ref, held, sems, tile, step, slot):
            copy.start()

    @pl.when(step + 1 < steps)
    def _():
        for copy in tile_copies(a_ref, held, sems, tile, step + 1, 1 - slot):
            copy.start()

    return slot, tile_copies(a_ref, held, sems, tile, step, slot)


def transposed_left(left, right):
    return lax.dot_general(
        left, right, (((0,), (0,)), ((), ())), preferred_element_type=jnp.float32
    )


def three_term(left, right, dot):
    high, low = left
    width = right.shape[1] // 2
    wide = dot(high, right)
    return wide[:, width:] + dot(low, right[:, :width]) + wide[:, :width]


def panel_kernel(first, group, mirrors, later, root_strip, *refs):
    refs = list(refs)
    take = lambda n: [refs.pop(0) for _ in range(n)]
    a_ref, cols_ref, lower_ref, top_ref = take(4)
    if later:
        old_cols_ref, old_rows_ref = take(2)
    if root_strip is not None:
        (strip_ref,) = take(1)
    w_ref, inverse_ref, rows_ref, spread_ref = take(4)
    if root_strip is not None:
        (strip_out,) = take(1)
    held, weights, part, arrived, sems = take(5)
    sum_send, sum_recv, on_send, on_recv, tree_send, tree_recv, local_sem = take(7)
    if later:
        small_ref, old_weights = take(2)
    rows, cols = lax.axis_size("row"), lax.axis_size("col")
    row, col = lax.axis_index("row"), lax.axis_index("col")
    cyc_cols, width = a_ref.shape[1:]
    pieces, tile = part.shape[1:3]
    tiles = cols * pieces
    greet("row", "col")

    def owner(index):
        return (col + 1 + index // pieces) % cols

    def fetch(index, slot):
        start = (owner(index) * pieces + index % pieces) * tile
        return [
            pltpu.make_async_copy(
                a_ref.at[pl.ds(pl.multiple_of(start, tile), tile), c, :],
                held.at[slot, c],
                sems.at[slot, c],
            )
            for c in range(cyc_cols)
        ]

    for copy in fetch(0, 0):
        copy.start()
    strip = None
    if root_strip is not None:
        root, layer = root_strip
        strip = Strip(root, strip_ref.at[layer], strip_out, *refs)
        strip.begin()

    square_row = lax.broadcasted_iota(jnp.int32, (width, width), 0)
    square_lane = lax.broadcasted_iota(jnp.int32, (width, width), 1)
    identity = (square_row == square_lane).astype(jnp.float32)
    if later:
        small_ref[...] = jnp.zeros_like(small_ref)

    @pl.loop(0, cyc_cols)
    def _(c):
        where = pl.ds(pl.multiple_of(c * width, width), width)
        w = transposed_dot(cols_ref[where, :], lower_ref[...])
        w = w - identity * (c * cols + col == first).astype(jnp.float32)
        w_ref[where, :] = w
        high, low = split(w)
        both = jnp.concatenate([high, low], axis=1)
        weights[where, :] = both
        if later:
            small_ref[...] += three_term(split(old_cols_ref[where, :]), both, transposed_left)

    if later:
        high, low = split(small_ref[...])
        old_weights[:, :width] = high
        old_weights[:, width:] = low

    def to_owner(index):
        q, piece = owner(index), index % pieces
        return remote(
            part.at[q, piece],
            arrived.at[index // pieces, piece],
            sum_send.at[index],
            sum_recv.at[index],
            col=q,
        )

    @pl.loop(0, tiles)
    def _(index):
        slot = lax.rem(index, 2)

        @pl.when(index + 1 < tiles)
        def _():
            for copy in fetch(index + 1, 1 - slot):
                copy.start()

        for copy in fetch(index, slot):
            copy.wait()
        total = None
        for chunk in range(cyc_cols // group):
            parts = [split(held[slot, chunk * group + g]) for g in range(group)]
            left = tuple(jnp.concatenate([p[i] for p in parts], axis=1) for i in range(2))
            right = weights[chunk * group * width : (chunk + 1) * group * width, :]
            term = three_term(left, right, dot_f32)
            total = term if total is None else total + term
        q, piece = owner(index), index % pieces
        if later:
            start = pl.multiple_of((q * pieces + piece) * tile, tile)
            old = split(old_rows_ref[pl.ds(start, tile), :])
            total = total - three_term(old, old_weights[...], dot_f32)
        part[q, piece] = total

        @pl.when(index < tiles - pieces)
        def _():
            to_owner(index).start()

        if strip is not None:
            strip.serve_turn(index)

    if strip is not None:

        @pl.loop(tiles, max(tiles, strip.turns()))
        def _(turn):
            strip.serve_turn(turn)

    inverse_ref[...] = -top_ref[...]
    eliminate(inverse_ref, False)

    bits = rows.bit_length() - 1
    order = list(range(1, bits)) + [0]
    across = [row + (1 - 2 * ((row // 2**b) % 2)) * 2**b for b in order]

    def spot(mirror, q, piece):
        start = (q * pieces + piece) * tile
        if tile >= width:
            blocks = tile // width
            return spread_ref.at[pl.ds((q * pieces + piece) * blocks, blocks), mirror]
        inside = pl.ds(pl.multiple_of(start % width, tile), tile)
        return spread_ref.at[start // width, mirror, inside]

    def source(q, piece):
        view = rows_ref.at[q, piece]
        return view.reshape(tile // width, width, width) if tile >= width else view

    def onward(q, piece, side):
        return remote(
            rows_ref.at[q, piece],
            rows_ref.at[q, piece],
            on_send.at[side, q, piece],
            on_recv.at[q, piece],
            col=(col + 1 - 2 * side + cols) % cols,
        )

    def branch(mirror, q, piece, t, view):
        return remote(
            view,
            spot(mirror, q, piece),
            tree_send.at[mirror, q, piece, t],
            tree_recv.at[mirror, q, piece],
            row=across[t],
        )

    def own_copy(mirror, q, piece):
        return pltpu.make_async_copy(
            source(q, piece), spot(mirror, q, piece), local_sem.at[mirror, q, piece]
        )

    below = []
    for mirror in range(mirrors):
        root = col + mirror * cols
        differ = [((row // 2**b) % 2 + (root // 2**b) % 2) % 2 for b in order]
        below.append([sum(differ[t:]) for t in range(bits)])

    def root_start(q, piece):
        for mirror in range(mirrors):

            @pl.when(below[mirror][0] == 0)
            def _():
                own_copy(mirror, q, piece).start()
                for t in range(bits):
                    branch(mirror, q, piece, t, source(q, piece)).start()

    def relay(mirror, q, piece):
        for t in range(bits):
            copy = branch(mirror, q, piece, t, spot(mirror, q, piece))
            if t == 0:
                copy.wait_recv()

            @pl.when(below[mirror][t] == 0)
            def _():
                copy.start()

    @pl.loop(0, pieces)
    def _(piece):
        value = part[col, piece]
        for step in range(cols - 1):
            to_owner(step * pieces + piece).wait_recv()
            value = value + arrived[step, piece]
        rows_ref[col, piece] = value
        for side in range(2):

            @pl.when((col < cols - 1) if side == 0 else (col > 0))
            def _():
                onward(col, piece, side).start()

    both_sides = jnp.minimum(col, cols - 1 - col)
    longer = jnp.where(2 * col < cols - 1, 1, -1)

    def visit(number):
        group, piece = number // pieces, number % pieces
        paired = group <= 2 * both_sides
        far = jnp.where(paired, (group + 1) // 2, group - both_sides)
        way = jnp.where(paired, 1 - 2 * (group % 2), longer)
        return col + far * way, piece, way

    visits = cols * pieces
    lags = [LAG * below[mirror][0] for mirror in range(mirrors)]

    @pl.loop(0, visits + LAG * bits)
    def _(number):
        q, piece, way = visit(number)

        @pl.when(number < visits)
        def _():
            for side in range(2):

                @pl.when((number >= pieces) & (way == 1 - 2 * (1 - side)))
                def _():
                    copy = onward(q, piece, side)
                    copy.wait_recv()

                    @pl.when((col < cols - 1) if side == 0 else (col > 0))
                    def _():
                        copy.start()

            root_start(q, piece)

        for mirror in range(mirrors):
            late = number - lags[mirror]

            @pl.when((below[mirror][0] != 0) & (late >= 0) & (late < visits))
            def _():
                q, piece, _way = visit(late)
                relay(mirror, q, piece)

    @pl.loop(0, cols)
    def _(q):
        @pl.loop(0, pieces)
        def _(piece):
            @pl.when((q <= col) & (col < cols - 1))
            def _():
                onward(q, piece, 0).wait_send()

            @pl.when((q >= col) & (col > 0))
            def _():
                onward(q, piece, 1).wait_send()

            for mirror in range(mirrors):

                @pl.when(below[mirror][0] == 0)
                def _():
                    own_copy(mirror, q, piece).wait()

                for t in range(bits):

                    @pl.when(below[mirror][t] == 0)
                    def _():
                        branch(mirror, q, piece, t, spot(mirror, q, piece)).wait_send()

    @pl.loop(0, tiles - pieces)
    def _(index):
        to_owner(index).wait_send()

    if strip is not None:
        strip.end()


def panel_product(matrix, cols, lower, w_top, first, old, root_strip, collective_id):
    rows_size, cols_size = lax.axis_size("row"), lax.axis_size("col")
    mirrors = rows_size // cols_size
    bits = rows_size.bit_length() - 1
    cyc_rows, width, cyc_cols, _ = matrix.shape
    n_rows = cyc_rows * width
    depth = n_rows // cols_size
    tile = min(256, depth)
    pieces = depth // tile
    flat = matrix.reshape(n_rows, cyc_cols, width)
    vmem, anywhere = pl.BlockSpec(memory_space=pltpu.VMEM), pl.BlockSpec(memory_space=pl.ANY)
    f32, dma = jnp.float32, pltpu.SemaphoreType.DMA
    args, specs = [flat, cols, lower, w_top], [anywhere, vmem, vmem, vmem]
    if old is not None:
        args += list(old)
        specs += [vmem, vmem]
    out_shape = [
        jax.ShapeDtypeStruct(cols.shape, f32),
        jax.ShapeDtypeStruct((width, width), f32),
        jax.ShapeDtypeStruct((cols_size, pieces, tile, width), f32),
        jax.ShapeDtypeStruct((cyc_rows, mirrors, width, width), f32),
    ]
    scratch = [
        pltpu.VMEM((2, cyc_cols, tile, width), f32),
        pltpu.VMEM((cols.shape[0], 2 * width), jnp.bfloat16),
        pltpu.VMEM((cols_size, pieces, tile, width), f32),
        pltpu.VMEM((cols_size - 1, pieces, tile, width), f32),
        dma((2, cyc_cols)),
        dma((cols_size * pieces,)),
        dma((cols_size * pieces,)),
        dma((2, cols_size, pieces)),
        dma((cols_size, pieces)),
        dma((mirrors, cols_size, pieces, bits)),
        dma((mirrors, cols_size, pieces)),
        dma((mirrors, cols_size, pieces)),
    ]
    if old is not None:
        scratch += [
            pltpu.VMEM((2 * width, width), f32),
            pltpu.VMEM((2 * width, 2 * width), jnp.bfloat16),
        ]
    if root_strip is not None:
        args.append(matrix)
        specs.append(anywhere)
        out_shape.append(jax.ShapeDtypeStruct(matrix.shape[1:], f32))
        scratch += STRIP_SEMS
    return pl.pallas_call(
        functools.partial(
            panel_kernel, first, min(8, cyc_cols), mirrors, old is not None, root_strip
        ),
        out_shape=out_shape,
        in_specs=specs,
        out_specs=[vmem] * len(out_shape),
        scratch_shapes=scratch,
        compiler_params=remote_params(collective_id),
    )(*args)


def update_kernel(group, a_ref, u_ref, vh_ref, vl_ref, out_ref, held, done, sems, out_sems):
    tile = u_ref.shape[0]
    cyc_cols, width = a_ref.shape[1:]
    step, steps = pl.program_id(0), pl.num_programs(0)
    slot, copies = fetch_tiles(a_ref, held, sems, tile)
    high, low = split(u_ref[...])

    def stores(index, where):
        return [
            pltpu.make_async_copy(
                done.at[where, c],
                out_ref.at[pl.ds(index * tile, tile), c, :],
                out_sems.at[where, c],
            )
            for c in range(cyc_cols)
        ]

    @pl.when(step >= 2)
    def _():
        for copy in stores(step - 2, slot):
            copy.wait()

    for copy in copies:
        copy.wait()
    started = stores(step, slot)
    for chunk in range(cyc_cols // group):
        columns = slice(chunk * group * width, (chunk + 1) * group * width)
        v_high, v_low = vh_ref[:, columns], vl_ref[:, columns]
        delta = dot_f32(high, v_low) + dot_f32(low, v_high) + dot_f32(high, v_high)
        for g in range(group):
            c = chunk * group + g
            done[slot, c] = held[slot, c] - delta[:, g * width : (g + 1) * width]
            started[c].start()

    @pl.when(step == steps - 1)
    def _():
        for copy in stores(step, slot):
            copy.wait()

        @pl.when(steps > 1)
        def _():
            for copy in stores(step - 1, 1 - slot):
                copy.wait()


def apply_update(matrix, left, right):
    cyc_rows, width, cyc_cols, _ = matrix.shape
    n_rows, depth = left.shape
    tile = min(256, n_rows)
    high, low = split_outside(right.T)
    whole = pl.BlockSpec(high.shape, lambda i: (0, 0), pipeline_mode=pl.Buffered(1))
    held = pltpu.VMEM((2, cyc_cols, tile, width), jnp.float32)
    sems = pltpu.SemaphoreType.DMA((2, cyc_cols))
    return pl.pallas_call(
        functools.partial(update_kernel, min(4, cyc_cols)),
        grid=(n_rows // tile,),
        out_shape=jax.ShapeDtypeStruct((n_rows, cyc_cols, width), jnp.float32),
        in_specs=[
            pl.BlockSpec(memory_space=pl.ANY),
            pl.BlockSpec((tile, depth), lambda i: (i, 0)),
            whole,
            whole,
        ],
        out_specs=pl.BlockSpec(memory_space=pl.ANY),
        scratch_shapes=[held, held, sems, sems],
        compiler_params=pltpu.CompilerParams(vmem_limit_bytes=VMEM_LIMIT),
    )(matrix.reshape(n_rows, cyc_cols, width), left, high, low)


def carry_rows(matrix, count):
    own = matrix[:, :, 0, :].reshape(-1, matrix.shape[3])
    col = lax.axis_index("col")
    last = max(count - 1, 3)
    kept = [own, own]
    moving = own
    for step in range(1, last + 1):
        pairs = [(i, i + 1) for i in (step - 1, step) if i + 1 < count]
        if step == last:
            pairs.append((1, 0))
            moving = jnp.where(col == 1, own, moving)
        moving = lax.ppermute(moving, "col", pairs)
        kept[0] = jnp.where(col == step, moving, kept[0])
        kept[1] = jnp.where(col == step + 1, moving, kept[1])
        if step == last:
            kept[1] = jnp.where(col == 0, moving, kept[1])
    return kept


def local(matrix):
    row_count = lax.axis_size("row")
    col_count = lax.axis_size("col")
    row_index = lax.axis_index("row")
    col_index = lax.axis_index("col")
    cyc_rows, width, cyc_cols, _ = matrix.shape
    n_rows, n_cols = cyc_rows * width, cyc_cols * width
    lanes = jnp.arange(width, dtype=jnp.int32)
    glob_rows = (
        (jnp.arange(cyc_rows, dtype=jnp.int32)[:, None] * row_count + row_index) * width + lanes
    ).reshape(-1)
    glob_cols = (
        (jnp.arange(cyc_cols, dtype=jnp.int32)[:, None] * col_count + col_index) * width + lanes
    ).reshape(-1)

    def columns_of(strip):
        return jnp.transpose(strip, (1, 2, 0)).reshape(n_cols, width)

    raw_rows = carry_rows(matrix, col_count)
    strip = spread_strip(matrix, 0, 0, 0)

    w_rows, w_cols, z_rows, z_cols = [], [], [], []
    w_next, z_next = [], []
    for k in range(PANELS):
        first = (k + 1) * width
        cols, rows = columns_of(strip), raw_rows[k]
        if k:
            inner = jnp.concatenate([w_next[0], z_next[0]], axis=1).T
            cols = cols - dot_highest(jnp.concatenate([z_cols[0], w_cols[0]], axis=1), inner)
            rows = rows - dot_highest(jnp.concatenate([z_rows[0], w_rows[0]], axis=1), inner)
        cols = jnp.where((glob_cols >= first)[:, None], cols, 0.0)
        rows = jnp.where((glob_rows >= first)[:, None], rows, 0.0)
        top_at = ((k + 1) // col_count) * width
        holds_top = col_index == (k + 1) % col_count
        top_part = jnp.where(holds_top, cols[top_at : top_at + width], 0.0)
        both = total(jnp.concatenate([dot_highest(cols.T, cols), top_part], axis=0), 1)
        inv_lower, w_top = factorize(both)
        unit_rows = (glob_rows[:, None] - first == lanes[None, :]).astype(jnp.float32)
        wr = dot_highest(rows, inv_lower.T) - unit_rows
        old = None
        if k:
            old = (
                jnp.concatenate([w_cols[0], z_cols[0]], axis=1),
                jnp.concatenate([z_rows[0], w_rows[0]], axis=1),
            )
        strip_of = ((k + 1) % row_count, (k + 1) // row_count) if k + 1 < PANELS else None
        wc, inverse, y_rows, y_cols, *rest = panel_product(
            matrix, cols, inv_lower, w_top, k + 1, old, strip_of, 2 + k
        )
        strip = rest[0] if rest else None
        y_rows = y_rows.reshape(n_rows, width)
        y_cols = y_cols.reshape(n_cols, width)
        next_part = jnp.where(holds_top, y_cols[top_at : top_at + width], 0.0)
        both = total(jnp.concatenate([dot_highest(wc.T, y_cols), next_part], axis=0), 1)
        middle, y_next = both[:width], both[width:]
        core = 0.5 * dot_highest(dot_highest(inverse, middle), inverse.T)
        finish = jnp.concatenate([inverse.T, -core], axis=0)
        w_rows.append(wr)
        w_cols.append(wc)
        w_next.append(w_top)
        z_rows.append(dot_highest(jnp.concatenate([y_rows, wr], axis=1), finish))
        z_cols.append(dot_highest(jnp.concatenate([y_cols, wc], axis=1), finish))
        z_next.append(dot_highest(jnp.concatenate([y_next, w_top], axis=1), finish))

    left = jnp.concatenate([x for k in range(PANELS) for x in (z_rows[k], w_rows[k])], axis=1)
    right = jnp.concatenate([x for k in range(PANELS) for x in (w_cols[k], z_cols[k])], axis=1)
    reduced = apply_update(matrix, left, right).reshape(matrix.shape)
    bases = jnp.concatenate(w_rows, axis=1).reshape(cyc_rows, width, PANELS * width)
    return (reduced, bases)


def solution(mesh):
    return jax.shard_map(
        local,
        mesh=mesh,
        in_specs=(P(None, "row", None, "col"),),
        out_specs=(P(None, "row", None, "col"), P(None, "row", None)),
        check_vma=False,
    )
```

profile of v0, /device:TPU:0, one launch (start us, length us, event | category | flops | bytes accessed | tf_op | source)
XLA Modules:
  0.0 411.9 jit_solution(9024232750040631216)
XLA Ops:
  0.6 4.0 slice.34
  4.7 6.0 %collective-permute-start = (f32[2048,128]{1,0:T(8,128)S(1)}, f32[2048,128]{1,0:T(8,128)}, u32[]{:S(2)}, u32[]{:S(2)}) collective-permute-start(f32[2048,128]{1,0:T(8,128)S(1)} %bitcast.66), channel_id=1, source_target_pairs={{0,1},{1,2},{4,5},{5,6},{8,9},{9,10},{12,13},{13,14},{16,17},{17,1... | collective-permute-start | bytes 3145736 | tf_op jit(solution)/shard_map/ppermute | solution.py:802
  10.7 16.8 %shard_map.30 = f32[128,32,128]{2,1,0:T(8,128)} custom-call(f32[16,128,32,128]{3,2,1,0:T(8,128)} %refs_4_.1), custom_call_target="tpu_custom_call" | custom-call | tf_op jit(solution)/shard_map/pallas_call | solution.py:183
  27.5 0.1 fusion.47
  27.6 1.8 broadcast_select_fusion
  29.5 4.2 %fusion.15 = f32[128,128]{1,0:T(8,128)S(1)} fusion(f32[32,128,128]{1,0,2:T(8,128)S(1)} %broadcast_select_fusion), kind=kOutput, calls=%fused_computation.31 | convolution fusion | flops 805306368 | bytes 2162688 | tf_op jit(solution)/shard_map/dot_general | solution.py:16
  33.6 0.0 copy-done.3
  33.7 1.9 copy.3
  35.5 3.6 bitcast_select_fusion.refs_1_
  39.1 0.0 copy-start.9
  39.2 0.8 pad_maximum_fusion.12
  39.9 20.3 %shard_map.31 = f32[8,32,128]{2,1,0:T(8,128)} custom-call(f32[8,32,128]{2,1,0:T(8,128)} %bitcast.89), custom_call_target="tpu_custom_call" | custom-call | tf_op jit(solution)/shard_map/pallas_call | solution.py:236
  60.2 8.0 %shard_map.32 = (f32[128,128]{1,0:T(8,128)}, f32[128,128]{1,0:T(8,128)}) custom-call(f32[256,128]{1,0:T(8,128)} %bitcast.87), custom_call_target="tpu_custom_call" | custom-call | tf_op jit(solution)/shard_map/pallas_call | solution.py:337
  68.2 67.8 %shard_map.33 = (f32[4096,128]{1,0:T(8,128)}, f32[128,128]{1,0:T(8,128)}, f32[4,2,256,128]{3,2,1,0:T(8,128)}, f32[16,2,128,128]{3,2,1,0:T(8,128)}, f32[128,32,128]{2,1,0:T(8,128)}) custom-call(f32[2048,32,128]{2,1,0:T(8,128)} %bitcast.61, f32[4096,128]{1,0:T(8,128)} %copy-done.9, f32[128,128]{1,0:T(8,128)} %get-tuple-element.15.refs_2_, ...), custom_call_target="tpu_custom_call" | custom-call | tf_op jit(solution)/shard_map/pallas_call | solution.py:710
  136.0 0.0 copy-start.12
  136.0 5.8 %fusion.63 = f32[128,128]{1,0:T(8,128)S(1)} fusion(f32[4096,128]{1,0:T(8,128)} %get-tuple-element.19, f32[4096,128]{1,0:T(8,128)} %bitcast.73), kind=kOutput, calls=%fused_computation.99 | convolution fusion | flops 805306368 | bytes 4259840 | tf_op jit(solution)/shard_map/dot_general | solution.py:16
  141.9 0.8 slice_select_fusion.2
  142.7 0.7 pad_maximum_fusion.13
  143.4 15.2 %shard_map.34 = f32[8,32,128]{2,1,0:T(8,128)} custom-call(f32[8,32,128]{2,1,0:T(8,128)} %bitcast.90), custom_call_target="tpu_custom_call" | custom-call | tf_op jit(solution)/shard_map/pallas_call | solution.py:236
  158.5 0.9 fusion.62
  159.4 0.2 fusion.64
  159.7 0.3 fusion.19
  159.9 0.0 copy-start.16
  159.9 7.4 %fusion.2 = f32[4096,128]{0,1:T(8,128)} fusion(f32[4096,128]{1,0:T(8,128)S(1)} %copy-done, f32[4096,128]{1,0:T(8,128)} %bitcast.75, f32[128,128]{0,1:T(8,128)S(1)} %fusion.19, f32[128,128]{0,1:T(8,128)S(1)} %bitcast.79), kind=kOutput, calls=%fused_computation.8 | convolution fusion | flops 1611694080 | bytes 6422528 | tf_op jit(solution)/shard_map/dot_general | solution.py:16
  167.4 0.0 collective-permute-done
  167.4 1.9 collective-permute-start.1
  169.3 0.3 fusion.40
  169.6 2.9 copy.9
  172.4 3.0 copy.8
  175.4 5.3 %fusion.1.refs_1_ = f32[4096,128]{1,0:T(8,128)S(1)} fusion(f32[4096,128]{1,0:T(8,128)} %bitcast.76, f32[4096,128]{1,0:T(8,128)S(1)} %copy-done, f32[4096,128]{1,0:T(8,128)} %copy.9, pred[4096]{0:T(1024)(128)(4,1)S(1)} %get-tuple-element.38, f32[128,128]{1,0:T(8,128)S(1)} %fusion.40, f32[128,128]{1,0:T(8,128)S(1)} %copy-done.16), kind=kOutput, calls=%fused_computation.7 | convolution fusion | flops 1612742656 | bytes 8523776 | tf_op jit(solution)/shard_map/dot_general | solution.py:16
  180.7 3.5 fusion.65
  184.3 0.7 pad_maximum_fusion.16
  184.9 0.0 collective-permute-done.1
  184.9 2.3 broadcast_select_fusion.1
  187.2 1.7 collective-permute-start.2
  189.0 1.8 copy.17
  190.8 33.3 %shard_map.35 = f32[8,32,128]{2,1,0:T(8,128)} custom-call(f32[8,32,128]{2,1,0:T(8,128)} %bitcast.86), custom_call_target="tpu_custom_call" | custom-call | tf_op jit(solution)/shard_map/pallas_call | solution.py:236
  224.2 8.0 %shard_map.36 = (f32[128,128]{1,0:T(8,128)}, f32[128,128]{1,0:T(8,128)}) custom-call(f32[256,128]{1,0:T(8,128)} %bitcast.88), custom_call_target="tpu_custom_call" | custom-call | tf_op jit(solution)/shard_map/pallas_call | solution.py:337
  232.1 0.1 fusion.51
  232.2 0.1 add_bitcast_fusion
  232.3 3.9 pad_maximum_fusion.4.refs_4_
  236.2 0.0 collective-permute-done.2
  236.2 2.6 convolution_subtract_fusion.2
  238.9 1.8 fusion.10
  240.7 1.8 fusion.44
  242.5 3.6 convolution_subtract_fusion.1
  246.2 2.4 pad_maximum_fusion.8
  248.6 80.5 %shard_map.37 = (f32[4096,128]{1,0:T(8,128)}, f32[128,128]{1,0:T(8,128)}, f32[4,2,256,128]{3,2,1,0:T(8,128)}, f32[16,2,128,128]{3,2,1,0:T(8,128)}) custom-call(f32[2048,32,128]{2,1,0:T(8,128)} %bitcast.62, f32[4096,128]{1,0:T(8,128)} %copy-done.1, f32[128,128]{1,0:T(8,128)} %get-tuple-element.22.refs_2_, f32[128,128]{1,0:T(8,128)} %get-tuple-element.23.refs_3_, ...), custom_call_target="tpu_custom_call" | custom-call | tf_op jit(solution)/shard_map/pallas_call | solution.py:710
  329.0 0.8 slice_select_fusion
  329.9 5.8 %fusion.66 = f32[128,128]{1,0:T(8,128)S(1)} fusion(f32[4096,128]{1,0:T(8,128)} %get-tuple-element.26, f32[4096,128]{1,0:T(8,128)} %bitcast.71), kind=kOutput, calls=%fused_computation.102 | convolution fusion | flops 805306368 | bytes 4259840 | tf_op jit(solution)/shard_map/dot_general | solution.py:16
  335.7 1.8 copy.18
  337.5 0.7 pad_maximum_fusion.17
  338.2 14.5 %shard_map.38 = f32[8,32,128]{2,1,0:T(8,128)} custom-call(f32[8,32,128]{2,1,0:T(8,128)} %bitcast.91), custom_call_target="tpu_custom_call" | custom-call | tf_op jit(solution)/shard_map/pallas_call | solution.py:236
  352.7 0.8 slice.42
  353.5 0.2 fusion.67
  353.7 0.3 fusion.18
  354.0 6.2 %fusion.5 = f32[4096,128]{0,1:T(8,128)S(1)} fusion(f32[4096,128]{1,0:T(8,128)S(1)} %copy-done.2, f32[4096,128]{1,0:T(8,128)} %bitcast.72, f32[128,128]{0,1:T(8,128)S(1)} %fusion.18, f32[128,128]{0,1:T(8,128)S(1)} %bitcast.82), kind=kOutput, calls=%fused_computation.13 | convolution fusion | flops 1611694080 | bytes 6422528 | tf_op jit(solution)/shard_map/dot_general | solution.py:16
  360.3 1.8 fusion.9
  362.1 0.0 copy-start.11
  362.2 2.5 pad_maximum_fusion.5.u_ref
  364.6 1.2 copy-done.10
  365.9 0.6 copy-done.11
  366.5 4.3 %fusion = (bf16[512,4096]{1,0:T(8,128)(2,1)}, bf16[512,4096]{1,0:T(8,128)(2,1)}) fusion(f32[4096,128]{0,1:T(8,128)S(1)} %fusion.5, f32[4096,128]{0,1:T(8,128)S(1)} %copy-done.11, f32[4096,128]{0,1:T(8,128)S(1)} %copy-done.4, f32[4096,128]{0,1:T(8,128)S(1)} %copy-done.10), kind=kLoop, calls=%fused_computation.2 | loop fusion | flops 14680064 | bytes 16777216 | tf_op jit(solution)/shard_map/convert_element_type | solution.py:351
  370.8 40.8 %shard_map.39 = f32[2048,32,128]{2,1,0:T(8,128)} custom-call(f32[2048,32,128]{2,1,0:T(8,128)} %bitcast.63, f32[2048,512]{1,0:T(8,128)} %pad_maximum_fusion.5.u_ref, bf16[512,4096]{1,0:T(8,128)(2,1)} %get-tuple-element.29.vh_ref, bf16[512,4096]{1,0:T(8,128)(2,1)} %get-tuple-element.28.vl_ref), custom_call_target="tpu_custom_call" | custom-call | tf_op jit(solution)/shard_map/pallas_call | solution.py:775
  (35 shorter events, 0.1 us)
Async XLA Ops:
  4.7 162.7 %collective-permute-start = (f32[2048,128]{1,0:T(8,128)S(1)}, f32[2048,128]{1,0:T(8,128)}, u32[]{:S(2)}, u32[]{:S(2)}) collective-permute-start(f32[2048,128]{1,0:T(8,128)S(1)} %bitcast.66), channel_id=1, source_target_pairs={{0,1},{1,2},{4,5},{5,6},{8,9},{9,10},{12,13},{13,14},{16,17},{17,1... | collective-permute-start | bytes 3145736 | tf_op jit(solution)/shard_map/ppermute | solution.py:802
  29.5 4.2 %copy-start.3 = (f32[128,32,128]{2,1,0:T(8,128)S(1)}, f32[128,32,128]{2,1,0:T(8,128)}, u32[]{:S(2)}) copy-start(f32[128,32,128]{2,1,0:T(8,128)} %shard_map.30) | copy-start | bytes 6291460
  39.1 29.1 %copy-start.9 = (f32[4096,128]{1,0:T(8,128)}, f32[4096,128]{1,0:T(8,128)S(1)}, u32[]{:S(2)}) copy-start(f32[4096,128]{1,0:T(8,128)S(1)} %bitcast_select_fusion.refs_1_) | copy-start | bytes 6291460
  136.0 23.4 %copy-start.12 = (f32[128,128]{1,0:T(8,128)S(1)}, f32[128,128]{1,0:T(8,128)}, u32[]{:S(2)}) copy-start(f32[128,128]{1,0:T(8,128)} %get-tuple-element.18) | copy-start | bytes 196612
  136.0 23.9 %copy-start = (f32[4096,128]{1,0:T(8,128)S(1)}, f32[4096,128]{1,0:T(8,128)}, u32[]{:S(2)}) copy-start(f32[4096,128]{1,0:T(8,128)} %get-tuple-element.19) | copy-start | bytes 6291460
  159.9 9.3 %copy-start.16 = (f32[128,128]{1,0:T(8,128)S(1)}, f32[128,128]{1,0:T(8,128)}, u32[]{:S(2)}) copy-start(f32[128,128]{1,0:T(8,128)} %get-tuple-element.16.refs_3_) | copy-start | bytes 196612
  167.4 17.5 %collective-permute-start.1 = (f32[2048,128]{1,0:T(8,128)}, f32[2048,128]{1,0:T(8,128)}, u32[]{:S(2)}, u32[]{:S(2)}) collective-permute-start(f32[2048,128]{1,0:T(8,128)} %collective-permute-done), channel_id=1, source_target_pairs={{1,2},{2,3},{5,6},{6,7},{9,10},{10,11},{13,14},{14,15},{17,18},{18... | collective-permute-start | bytes 3145736 | tf_op jit(solution)/shard_map/ppermute | solution.py:802
  180.7 3.6 copy-start.1
  187.2 48.9 %collective-permute-start.2 = (f32[2048,128]{1,0:T(8,128)}, f32[2048,128]{1,0:T(8,128)}, u32[]{:S(2)}, u32[]{:S(2)}) collective-permute-start(f32[2048,128]{1,0:T(8,128)} %broadcast_select_fusion.1), channel_id=1, source_target_pairs={{2,3},{1,0},{6,7},{5,4},{10,11},{9,8},{14,15},{13,12},{18,19},{17,... | collective-permute-start | bytes 3145736 | tf_op jit(solution)/shard_map/ppermute | solution.py:802
  232.3 3.9 copy-start.18
  236.2 2.7 copy-start.14
  240.7 5.5 %copy-start.5 = (f32[2048,128]{1,0:T(8,128)}, f32[2048,128]{1,0:T(8,128)S(1)}, u32[]{:S(2)}) copy-start(f32[2048,128]{1,0:T(8,128)S(1)} %fusion.10) | copy-start | bytes 3145732
  240.7 1.9 copy-start.17
  246.1 2.4 copy-start.7
  329.9 5.8 %copy-start.2 = (f32[4096,128]{1,0:T(8,128)S(1)}, f32[4096,128]{1,0:T(8,128)}, u32[]{:S(2)}) copy-start(f32[4096,128]{1,0:T(8,128)} %get-tuple-element.26) | copy-start | bytes 6291460
  335.7 17.8 %copy-start.13 = (f32[128,128]{1,0:T(8,128)S(1)}, f32[128,128]{1,0:T(8,128)}, u32[]{:S(2)}) copy-start(f32[128,128]{1,0:T(8,128)} %get-tuple-element.25) | copy-start | bytes 196612
  354.0 6.2 %copy-start.8 = (f32[2048,128]{1,0:T(8,128)S(1)}, f32[2048,128]{1,0:T(8,128)}, u32[]{:S(2)}) copy-start(f32[2048,128]{1,0:T(8,128)} %copy-done.7) | copy-start | bytes 3145732
  354.0 6.2 %copy-start.15 = (f32[4,2,256,128]{3,2,1,0:T(8,128)S(1)}, f32[4,2,256,128]{3,2,1,0:T(8,128)}, u32[]{:S(2)}) copy-start(f32[4,2,256,128]{3,2,1,0:T(8,128)} %get-tuple-element.24) | copy-start | bytes 3145732
  360.2 1.9 copy-start.6
  362.1 2.5 copy-start.4
  362.1 3.7 copy-start.10
  362.1 4.4 %copy-start.11 = (f32[4096,128]{0,1:T(8,128)S(1)}, f32[4096,128]{0,1:T(8,128)}, u32[]{:S(2)}) copy-start(f32[4096,128]{0,1:T(8,128)} %copy.18) | copy-start | bytes 6291460
where the time goes:
time: 419 us; the launch traced here: 412 us
  Pallas kernels  305 us (73%)
  matrix products  51.2 us (12%)
  other arithmetic  25.5 us (6%)
  local copies, waits for them, and re-layouts  19.1 us (5%)
  starting transfers between devices  9.6 us (2%)
    pallas_call x2, Pallas kernels, panel_product(): pl.pallas_call(functools.partial(panel_kernel, first, min(8, cyc_cols), m...  148 us
    pallas_call x4, Pallas kernels, total(): pl.pallas_call(total_kernel, out_shape=jax.ShapeDtypeStruct(shape, x.dtyp...  83.2 us
    dot_general x17, matrix products, dot_highest(): jnp.dot(left, right, precision=lax.Precision.HIGHEST, preferred_element_t...  51.2 us
    pallas_call x1, Pallas kernels, apply_update(): pl.pallas_call(functools.partial(update_kernel, min(4, cyc_cols)), grid=(...  40.8 us
    pallas_call x1, Pallas kernels, spread_strip(): pl.pallas_call(functools.partial(strip_kernel, root, layer), out_shape=ja...  16.8 us
    pallas_call x2, Pallas kernels, factorize(): pl.pallas_call(factor_kernel, out_shape=[jax.ShapeDtypeStruct((width, wid...  15.9 us
    ppermute x3, starting transfers between devices, carry_rows(): moving = lax.ppermute(moving, 'col', pairs)  9.6 us
  transfers between devices with their start and end apart: 3, of which 0 were waited for; matrix products, arithmetic and copies ran while one was open for 12% of the time, Pallas kernels for 41%

commit v1 on v0

--- a/solution.py
+++ b/solution.py
@@ -166,36 +166,113 @@
 ]
 
 
-def strip_kernel(root, layer, a_ref, out_ref, *sems):
-    greet("row")
-    strip = Strip(root, a_ref.at[layer], out_ref, *sems)
+class Chain:
+    def __init__(self, root, layer, a_ref, out_ref, send, recv, local_sems):
+        self.col, self.cols = lax.axis_index("col"), lax.axis_size("col")
+        self.root, self.layer, self.a_ref, self.out_ref = root, layer, a_ref, out_ref
+        self.send, self.recv, self.local_sems = send, recv, local_sems
+        self.count = recv.shape[0]
+        self.piece = out_ref.shape[0] // self.count
+        self.ways = [(self.col >= root) & (self.col < self.cols - 1), (self.col <= root) & (self.col > 0)]
+
+    def part(self, i):
+        return pl.ds(pl.multiple_of(i * self.piece, self.piece), self.piece)
+
+    def local(self, i):
+        return pltpu.make_async_copy(
+            self.a_ref.at[self.part(i), :, self.layer, :],
+            self.out_ref.at[self.part(i)],
+            self.local_sems.at[i],
+        )
+
+    def onward(self, i, side):
+        view = self.out_ref.at[self.part(i)]
+        target = (self.col + 1 - 2 * side + self.cols) % self.cols
+        return remote(view, view, self.send.at[side, i], self.recv.at[i], col=target)
+
+    def begin(self):
+        @pl.when(self.col == self.root)
+        def _():
+            for i in range(self.count):
+                self.local(i).start()
+            for i in range(self.count):
+                self.local(i).wait()
+                for side in range(2):
+
+                    @pl.when(self.ways[side])
+                    def _():
+                        self.onward(i, side).start()
+
+    def serve(self, i):
+        @pl.when(self.col != self.root)
+        def _():
+            self.onward(i, 0).wait_recv()
+            for side in range(2):
+
+                @pl.when(self.ways[side])
+                def _():
+                    self.onward(i, side).start()
+
+    def serve_turn(self, turn):
+        far = jnp.maximum(self.col - self.root, self.root - self.col)
+        i = turn - far
+
+        @pl.when((i >= 0) & (i < self.count))
+        def _():
+            self.serve(i)
+
+    def turns(self):
+        return self.count + self.cols
+
+    def end(self):
+        for i in range(self.count):
+            for side in range(2):
+
+                @pl.when(self.ways[side])
+                def _():
+                    self.onward(i, side).wait_send()
+
+
+def chain_sems(cyc_rows):
+    count = min(8, cyc_rows)
+    dma = pltpu.SemaphoreType.DMA
+    return [dma((2, count)), dma((count,)), dma((count,))]
+
+
+def spread_kernel(root, layer, col_root, col_layer, a_ref, strip_ref, rows_ref, *sems):
+    greet("row", "col")
+    strip = Strip(root, a_ref.at[layer], strip_ref, *sems[: len(STRIP_SEMS)])
+    chain = Chain(col_root, col_layer, a_ref, rows_ref, *sems[len(STRIP_SEMS) :])
     strip.begin()
-
-    @pl.when(strip.me != root)
-    def _():
-        for i in range(STREAM_CHUNKS):
-            strip.serve(i)
+    chain.begin()
+
+    @pl.loop(0, max(strip.turns(), chain.turns()))
+    def _(turn):
+        chain.serve_turn(turn)
+        strip.serve_turn(turn)
 
     strip.end()
-
-
-def spread_strip(matrix, root, layer, collective_id):
+    chain.end()
+
+
+def spread(matrix, root, layer, col_root, col_layer, collective_id):
+    cyc_rows, width, _, _ = matrix.shape
     return pl.pallas_call(
-        functools.partial(strip_kernel, root, layer),
-        out_shape=jax.ShapeDtypeStruct(matrix.shape[1:], matrix.dtype),
+        functools.partial(spread_kernel, root, layer, col_root, col_layer),
+        out_shape=[
+            jax.ShapeDtypeStruct(matrix.shape[1:], matrix.dtype),
+            jax.ShapeDtypeStruct((cyc_rows, width, width), matrix.dtype),
+        ],
         in_specs=[pl.BlockSpec(memory_space=pl.ANY)],
-        out_specs=pl.BlockSpec(memory_space=pltpu.VMEM),
-        scratch_shapes=STRIP_SEMS,
+        out_specs=[pl.BlockSpec(memory_space=pltpu.VMEM)] * 2,
+        scratch_shapes=STRIP_SEMS + chain_sems(cyc_rows),
         compiler_params=remote_params(collective_id),
     )(matrix)
 
 
-def total_kernel(x_ref, out_ref, held, col_send, col_recv, row_send, row_recv, local_sem):
+def sum_over_col(x_ref, out_ref, held, col_send, col_recv, row_send, row_recv, between=None):
     rows, cols = lax.axis_size("row"), lax.axis_size("col")
     row, col = lax.axis_index("row"), lax.axis_index("col")
-    greet("row", "col")
-    own = pltpu.make_async_copy(x_ref.at[row], held.at[col], local_sem)
-    own.start()
     copies = []
     for step in range(1, cols):
         copy = remote(
@@ -207,7 +284,7 @@
         )
         copy.start()
         copies.append(copy)
-    own.wait()
+    held[col] = x_ref[row]
     for copy in copies:
         copy.wait()
     value = held[0]
@@ -225,36 +302,41 @@
         )
         copy.start()
         copies.append(copy)
+    if between is not None:
+        between()
     for copy in copies:
         copy.wait()
 
 
-def total(x, collective_id):
+def sum_scratch(width):
     rows, cols = lax.axis_size("row"), lax.axis_size("col")
-    piece = x.shape[0] // rows
-    shape = (rows, piece, x.shape[1])
-    out = pl.pallas_call(
-        total_kernel,
-        out_shape=jax.ShapeDtypeStruct(shape, x.dtype),
-        in_specs=[pl.BlockSpec(memory_space=pltpu.VMEM)],
-        out_specs=pl.BlockSpec(memory_space=pltpu.VMEM),
-        scratch_shapes=[
-            pltpu.VMEM((cols, piece, x.shape[1]), x.dtype),
-            pltpu.SemaphoreType.DMA((cols,)),
-            pltpu.SemaphoreType.DMA((cols,)),
-            pltpu.SemaphoreType.DMA((rows,)),
-            pltpu.SemaphoreType.DMA((rows,)),
-            pltpu.SemaphoreType.DMA,
-        ],
-        compiler_params=remote_params(collective_id),
-    )(x.reshape(shape))
-    return out.reshape(x.shape)
+    piece = 2 * width // rows
+    dma = pltpu.SemaphoreType.DMA
+    return [
+        pltpu.VMEM((rows, piece, width), jnp.float32),
+        pltpu.VMEM((cols, piece, width), jnp.float32),
+        dma((cols,)),
+        dma((cols,)),
+        dma((rows,)),
+        dma((rows,)),
+    ]
+
+
+def put_half(x_ref, half, value):
+    rows, piece, width = x_ref.shape
+    for r in range(rows // 2):
+        x_ref[half * (rows // 2) + r] = value[r * piece : (r + 1) * piece]
+
+
+def get_half(x_ref, half):
+    rows, piece, width = x_ref.shape
+    return x_ref[pl.ds(half * (rows // 2), rows // 2)].reshape(width, width)
 
 
 LEAF = 16
 
 
-def eliminate(ref, symmetric):
+def eliminate(ref, symmetric, beside=None):
     size = ref.shape[0]
     strip_row = lax.broadcasted_iota(jnp.int32, (LEAF, size), 0)
     strip_lane = lax.broadcasted_iota(jnp.int32, (LEAF, size), 1)
@@ -305,6 +387,8 @@
             ref[...] = base - dot_highest(factor, padded)
         ref[pl.ds(start, LEAF), :] = panel
         ref[...] = pltpu.roll(ref[...], size - LEAF, axis=1)
+        if beside is not None:
+            beside(b)
         return carry
 
     lax.fori_loop(0, size // LEAF, block, 0)
@@ -322,33 +406,9 @@
     )
 
 
-def factor_kernel(both_ref, lower_ref, top_ref):
-    width = both_ref.shape[1]
-    lower_ref[...] = both_ref[:width]
-    eliminate(lower_ref, True)
-    row = lax.broadcasted_iota(jnp.int32, (width, width), 0)
-    lane = lax.broadcasted_iota(jnp.int32, (width, width), 1)
-    identity = (row == lane).astype(jnp.float32)
-    top_ref[...] = transposed_dot(both_ref[width:], lower_ref[...]) - identity
-
-
-def factorize(both):
-    width = both.shape[1]
-    return pl.pallas_call(
-        factor_kernel,
-        out_shape=[jax.ShapeDtypeStruct((width, width), jnp.float32)] * 2,
-        compiler_params=pltpu.CompilerParams(vmem_limit_bytes=VMEM_LIMIT),
-    )(both)
-
-
 def split(value):
     high = value.astype(jnp.bfloat16)
     return high, (value - high.astype(jnp.float32)).astype(jnp.bfloat16)
-
-
-def split_outside(value):
-    high = lax.reduce_precision(value, exponent_bits=8, mantissa_bits=7)
-    return high.astype(jnp.bfloat16), (value - high).astype(jnp.bfloat16)
 
 
 def dot_f32(left, right):
@@ -394,19 +454,183 @@
     return wide[:, width:] + dot(low, right[:, :width]) + wide[:, :width]
 
 
+def eye(width):
+    row = lax.broadcasted_iota(jnp.int32, (width, width), 0)
+    lane = lax.broadcasted_iota(jnp.int32, (width, width), 1)
+    return (row == lane).astype(jnp.float32)
+
+
+def flag(condition):
+    return condition.astype(jnp.float32)
+
+
+def side_by_side(value):
+    return jnp.concatenate(split(value), axis=1)
+
+
+def prepare_kernel(first, later, chain_root, *refs):
+    refs = list(refs)
+    take = lambda n: [refs.pop(0) for _ in range(n)]
+    strip_ref, raw_rows_ref = take(2)
+    if later:
+        both_ref, inverse_ref, old_top_ref, y_cols_ref, w_cols_ref, y_rows_ref, w_rows_ref = take(7)
+    if chain_root is not None:
+        (a_ref,) = take(1)
+    cols_ref, rows_ref, lower_ref, top_ref = take(4)
+    if later:
+        old_cols_ref, old_rows_ref = take(2)
+    if chain_root is not None:
+        (chain_ref,) = take(1)
+    total_ref, summed_ref, gram_ref = take(3)
+    sums = take(5)
+    rows, cols = lax.axis_size("row"), lax.axis_size("col")
+    row, col = lax.axis_index("row"), lax.axis_index("col")
+    width = lower_ref.shape[0]
+    cyc_cols, cyc_rows = strip_ref.shape[1], raw_rows_ref.shape[0]
+    greet("row", "col")
+    chain = None
+    if chain_root is not None:
+        chain = Chain(*chain_root, a_ref, chain_ref, *refs)
+        chain.begin()
+
+    if later:
+        inverse = inverse_ref[...]
+        middle, y_next = get_half(both_ref, 0), get_half(both_ref, 1)
+        core = 0.5 * transposed_dot(dot_highest(inverse, middle), inverse)
+        z_next = transposed_dot(y_next, inverse) - dot_highest(old_top_ref[...], core)
+        finish = side_by_side(jnp.concatenate([inverse.T, -core], axis=0))
+        inner = side_by_side(jnp.concatenate([old_top_ref[...].T, z_next.T], axis=0))
+
+    def old_pair(y, w):
+        return three_term(split(jnp.concatenate([y, w], axis=1)), finish, dot_f32)
+
+    def correction(z, w):
+        return three_term(split(jnp.concatenate([z, w], axis=1)), inner, dot_f32)
+
+    gram_ref[...] = jnp.zeros_like(gram_ref)
+    step = min(4, cyc_cols)
+    for group in range(cyc_cols // step):
+        where = slice(group * step * width, (group + 1) * step * width)
+        held = range(group * step, (group + 1) * step)
+        tall = jnp.concatenate([strip_ref[:, c, :].T for c in held], axis=0)
+        if later:
+            w = w_cols_ref[where, :]
+            z = old_pair(y_cols_ref[where, :], w)
+            old_cols_ref[where, :width] = w
+            old_cols_ref[where, width:] = z
+            tall = tall - correction(z, w)
+        if group * step * cols < first:
+            blocks = [
+                jnp.where(c * cols + col >= first, tall[i * width : (i + 1) * width], 0.0)
+                for i, c in enumerate(held)
+            ]
+            tall = jnp.concatenate(blocks, axis=0)
+        cols_ref[where, :] = tall
+        gram_ref[...] += lax.dot_general(
+            tall,
+            tall,
+            (((0,), (0,)), ((), ())),
+            precision=lax.Precision.HIGHEST,
+            preferred_element_type=jnp.float32,
+        )
+        if chain is not None and group % 2 == 1:
+            chain.serve_turn(group // 2)
+    served = (cyc_cols // step) // 2
+    put_half(total_ref, 0, gram_ref[...])
+    top_at = (first // cols) * width
+    holds = col == first % cols
+    put_half(total_ref, 1, jnp.where(holds, cols_ref[top_at : top_at + width, :], 0.0))
+
+    def own_rows():
+        for group in range(cyc_rows // 4):
+            where = slice(group * 4 * width, (group + 1) * 4 * width)
+            tall = raw_rows_ref[group * 4 : (group + 1) * 4].reshape(4 * width, width)
+            if later:
+                w = w_rows_ref[where, :]
+                z = old_pair(y_rows_ref[where, :], w)
+                old_rows_ref[where, :width] = z
+                old_rows_ref[where, width:] = w
+                tall = tall - correction(z, w)
+            for i in range(4):
+                block = tall[i * width : (i + 1) * width]
+                at = group * 4 + i
+                if at * rows < first:
+                    block = jnp.where(at * rows + row >= first, block, 0.0)
+                rows_ref[at * width : (at + 1) * width, :] = block
+        if chain is not None:
+            chain.serve_turn(served)
+
+    sum_over_col(total_ref, summed_ref, *sums, between=own_rows)
+    lower_ref[...] = get_half(summed_ref, 0)
+
+    def beside(b):
+        if chain is not None:
+
+            @pl.when(b % 2 == 1)
+            def _():
+                chain.serve_turn(served + 1 + b // 2)
+
+    eliminate(lower_ref, True, beside)
+    top_ref[...] = transposed_dot(get_half(summed_ref, 1), lower_ref[...]) - eye(width)
+    if chain is not None:
+
+        @pl.loop(served + 1 + width // LEAF // 2, chain.turns())
+        def _(turn):
+            chain.serve_turn(turn)
+
+        chain.end()
+
+
+def prepare(strip, raw_rows, first, later, matrix, chain_root, collective_id):
+    width, cyc_cols, _ = strip.shape
+    cyc_rows = raw_rows.shape[0]
+    f32, vmem = jnp.float32, pl.BlockSpec(memory_space=pltpu.VMEM)
+    square = jax.ShapeDtypeStruct((width, width), f32)
+    args = [strip, raw_rows]
+    out_shape = [
+        jax.ShapeDtypeStruct((cyc_cols * width, width), f32),
+        jax.ShapeDtypeStruct((cyc_rows * width, width), f32),
+        square,
+        square,
+    ]
+    if later is not None:
+        args += later
+        out_shape += [
+            jax.ShapeDtypeStruct((cyc_cols * width, 2 * width), f32),
+            jax.ShapeDtypeStruct((cyc_rows * width, 2 * width), f32),
+        ]
+    specs = [vmem] * len(args)
+    sums = sum_scratch(width)
+    scratch = [sums[0], sums[0], pltpu.VMEM((width, width), f32)] + sums[1:]
+    if chain_root is not None:
+        args.append(matrix)
+        specs.append(pl.BlockSpec(memory_space=pl.ANY))
+        out_shape.append(jax.ShapeDtypeStruct((cyc_rows, width, width), f32))
+        scratch += chain_sems(cyc_rows)
+    return pl.pallas_call(
+        functools.partial(prepare_kernel, first, later is not None, chain_root),
+        out_shape=out_shape,
+        in_specs=specs,
+        out_specs=[vmem] * len(out_shape),
+        scratch_shapes=scratch,
+        compiler_params=remote_params(collective_id),
+    )(*args)
+
+
 def panel_kernel(first, group, mirrors, later, root_strip, *refs):
     refs = list(refs)
     take = lambda n: [refs.pop(0) for _ in range(n)]
-    a_ref, cols_ref, lower_ref, top_ref = take(4)
+    a_ref, cols_ref, lower_ref, top_ref, own_ref = take(5)
     if later:
         old_cols_ref, old_rows_ref = take(2)
     if root_strip is not None:
         (strip_ref,) = take(1)
-    w_ref, inverse_ref, rows_ref, spread_ref = take(4)
+    w_ref, inverse_ref, rows_ref, spread_ref, w_rows_ref, both_ref = take(6)
     if root_strip is not None:
         (strip_out,) = take(1)
     held, weights, part, arrived, sems = take(5)
     sum_send, sum_recv, on_send, on_recv, tree_send, tree_recv, local_sem = take(7)
+    total_ref, *sums = take(6)
     if later:
         small_ref, old_weights = take(2)
     rows, cols = lax.axis_size("row"), lax.axis_size("col")
@@ -444,14 +668,18 @@
     if later:
         small_ref[...] = jnp.zeros_like(small_ref)
 
-    @pl.loop(0, cyc_cols)
-    def _(c):
-        where = pl.ds(pl.multiple_of(c * width, width), width)
+    tall = min(4, cyc_cols)
+
+    @pl.loop(0, cyc_cols // tall)
+    def _(chunk):
+        where = pl.ds(pl.multiple_of(chunk * tall * width, tall * width), tall * width)
         w = transposed_dot(cols_ref[where, :], lower_ref[...])
-        w = w - identity * (c * cols + col == first).astype(jnp.float32)
+        units = [
+            identity * flag((chunk * tall + c) * cols + col == first) for c in range(tall)
+        ]
+        w = w - jnp.concatenate(units, axis=0)
         w_ref[where, :] = w
-        high, low = split(w)
-        both = jnp.concatenate([high, low], axis=1)
+        both = side_by_side(w)
         weights[where, :] = both
         if later:
             small_ref[...] += three_term(split(old_cols_ref[where, :]), both, transposed_left)
@@ -511,6 +739,11 @@
 
     inverse_ref[...] = -top_ref[...]
     eliminate(inverse_ref, False)
+    for chunk in range(own_ref.shape[0] // (4 * width)):
+        where = slice(chunk * 4 * width, (chunk + 1) * 4 * width)
+        w = transposed_dot(own_ref[where, :], lower_ref[...])
+        units = [identity * flag((chunk * 4 + i) * rows + row == first) for i in range(4)]
+        w_rows_ref[where, :] = w - jnp.concatenate(units, axis=0)
 
     bits = rows.bit_length() - 1
     order = list(range(1, bits)) + [0]
@@ -657,11 +890,23 @@
     def _(index):
         to_owner(index).wait_send()
 
+    small = jnp.zeros((width, width), jnp.float32)
+    for chunk in range(cyc_cols // tall):
+        where = slice(chunk * tall * width, (chunk + 1) * tall * width)
+        y = spread_ref[chunk * tall // mirrors : (chunk + 1) * tall // mirrors]
+        y = y.reshape(tall * width, width)
+        small = small + three_term(split(y), weights[where, :], transposed_left)
+    put_half(total_ref, 0, small.T)
+    c = first // cols
+    y = spread_ref[c // mirrors, c % mirrors]
+    put_half(total_ref, 1, jnp.where(col == first % cols, y, 0.0))
+    sum_over_col(total_ref, both_ref, *sums)
+
     if strip is not None:
         strip.end()
 
 
-def panel_product(matrix, cols, lower, w_top, first, old, root_strip, collective_id):
+def panel_product(matrix, cols, lower, w_top, own, first, old, root_strip, collective_id):
     rows_size, cols_size = lax.axis_size("row"), lax.axis_size("col")
     mirrors = rows_size // cols_size
     bits = rows_size.bit_length() - 1
@@ -673,7 +918,7 @@
     flat = matrix.reshape(n_rows, cyc_cols, width)
     vmem, anywhere = pl.BlockSpec(memory_space=pltpu.VMEM), pl.BlockSpec(memory_space=pl.ANY)
     f32, dma = jnp.float32, pltpu.SemaphoreType.DMA
-    args, specs = [flat, cols, lower, w_top], [anywhere, vmem, vmem, vmem]
+    args, specs = [flat, cols, lower, w_top, own], [anywhere, vmem, vmem, vmem, vmem]
     if old is not None:
         args += list(old)
         specs += [vmem, vmem]
@@ -682,6 +927,8 @@
         jax.ShapeDtypeStruct((width, width), f32),
         jax.ShapeDtypeStruct((cols_size, pieces, tile, width), f32),
         jax.ShapeDtypeStruct((cyc_rows, mirrors, width, width), f32),
+        jax.ShapeDtypeStruct((n_rows, width), f32),
+        jax.ShapeDtypeStruct((rows_size, 2 * width // rows_size, width), f32),
     ]
     scratch = [
         pltpu.VMEM((2, cyc_cols, tile, width), f32),
@@ -696,7 +943,7 @@
         dma((mirrors, cols_size, pieces, bits)),
         dma((mirrors, cols_size, pieces)),
         dma((mirrors, cols_size, pieces)),
-    ]
+    ] + sum_scratch(width)
     if old is not None:
         scratch += [
             pltpu.VMEM((2 * width, width), f32),
@@ -719,12 +966,14 @@
     )(*args)
 
 
-def update_kernel(group, a_ref, u_ref, vh_ref, vl_ref, out_ref, held, done, sems, out_sems):
-    tile = u_ref.shape[0]
+def update_kernel(
+    group, a_ref, uh_ref, ul_ref, vh_ref, vl_ref, out_ref, held, done, sems, out_sems
+):
+    tile = uh_ref.shape[0]
     cyc_cols, width = a_ref.shape[1:]
     step, steps = pl.program_id(0), pl.num_programs(0)
     slot, copies = fetch_tiles(a_ref, held, sems, tile)
-    high, low = split(u_ref[...])
+    high, low = uh_ref[...], ul_ref[...]
 
     def stores(index, where):
         return [
@@ -764,117 +1013,102 @@
                 copy.wait()
 
 
-def apply_update(matrix, left, right):
+def finish_kernel(
+    both_ref, inverse_ref, y_cols_ref, w_cols_ref, y_rows_ref, w_rows_ref,
+    old_cols_ref, old_rows_ref, lh_ref, ll_ref, rh_ref, rl_ref,
+):
+    width = inverse_ref.shape[0]
+    inverse = inverse_ref[...]
+    core = 0.5 * transposed_dot(dot_highest(inverse, get_half(both_ref, 0)), inverse)
+    finish = side_by_side(jnp.concatenate([inverse.T, -core], axis=0))
+    step = 4 * width
+
+    @pl.loop(0, y_rows_ref.shape[0] // step)
+    def _(group):
+        where = pl.ds(pl.multiple_of(group * step, step), step)
+        w = w_rows_ref[where, :]
+        z = three_term(
+            split(jnp.concatenate([y_rows_ref[where, :], w], axis=1)), finish, dot_f32
+        )
+        for at, value in ((0, old_rows_ref[where, :]), (2 * width, z), (3 * width, w)):
+            high, low = split(value)
+            lh_ref[where, at : at + value.shape[1]] = high
+            ll_ref[where, at : at + value.shape[1]] = low
+
+    @pl.loop(0, y_cols_ref.shape[0] // step)
+    def _(group):
+        where = pl.ds(pl.multiple_of(group * step, step), step)
+        w = w_cols_ref[where, :]
+        z = three_term(
+            split(jnp.concatenate([y_cols_ref[where, :], w], axis=1)), finish, dot_f32
+        )
+        for at, value in ((0, old_cols_ref[where, :]), (2 * width, w), (3 * width, z)):
+            high, low = split(value.T)
+            rh_ref[at : at + value.shape[1], where] = high
+            rl_ref[at : at + value.shape[1], where] = low
+
+
+def finish_factors(both, inverse, y_cols, w_cols, y_rows, w_rows, old_cols, old_rows):
+    width = inverse.shape[0]
+    left = jax.ShapeDtypeStruct((y_rows.shape[0], 4 * width), jnp.bfloat16)
+    right = jax.ShapeDtypeStruct((4 * width, y_cols.shape[0]), jnp.bfloat16)
+    return pl.pallas_call(
+        finish_kernel,
+        out_shape=[left, left, right, right],
+        compiler_params=pltpu.CompilerParams(vmem_limit_bytes=VMEM_LIMIT),
+    )(both, inverse, y_cols, w_cols, y_rows, w_rows, old_cols, old_rows)
+
+
+def apply_update(matrix, left_high, left_low, high, low):
     cyc_rows, width, cyc_cols, _ = matrix.shape
-    n_rows, depth = left.shape
+    n_rows, depth = left_high.shape
     tile = min(256, n_rows)
-    high, low = split_outside(right.T)
     whole = pl.BlockSpec(high.shape, lambda i: (0, 0), pipeline_mode=pl.Buffered(1))
+    some = pl.BlockSpec((tile, depth), lambda i: (i, 0))
     held = pltpu.VMEM((2, cyc_cols, tile, width), jnp.float32)
     sems = pltpu.SemaphoreType.DMA((2, cyc_cols))
     return pl.pallas_call(
         functools.partial(update_kernel, min(4, cyc_cols)),
         grid=(n_rows // tile,),
         out_shape=jax.ShapeDtypeStruct((n_rows, cyc_cols, width), jnp.float32),
-        in_specs=[
-            pl.BlockSpec(memory_space=pl.ANY),
-            pl.BlockSpec((tile, depth), lambda i: (i, 0)),
-            whole,
-            whole,
-        ],
+        in_specs=[pl.BlockSpec(memory_space=pl.ANY), some, some, whole, whole],
         out_specs=pl.BlockSpec(memory_space=pl.ANY),
         scratch_shapes=[held, held, sems, sems],
         compiler_params=pltpu.CompilerParams(vmem_limit_bytes=VMEM_LIMIT),
-    )(matrix.reshape(n_rows, cyc_cols, width), left, high, low)
-
-
-def carry_rows(matrix, count):
-    own = matrix[:, :, 0, :].reshape(-1, matrix.shape[3])
-    col = lax.axis_index("col")
-    last = max(count - 1, 3)
-    kept = [own, own]
-    moving = own
-    for step in range(1, last + 1):
-        pairs = [(i, i + 1) for i in (step - 1, step) if i + 1 < count]
-        if step == last:
-            pairs.append((1, 0))
-            moving = jnp.where(col == 1, own, moving)
-        moving = lax.ppermute(moving, "col", pairs)
-        kept[0] = jnp.where(col == step, moving, kept[0])
-        kept[1] = jnp.where(col == step + 1, moving, kept[1])
-        if step == last:
-            kept[1] = jnp.where(col == 0, moving, kept[1])
-    return kept
+    )(matrix.reshape(n_rows, cyc_cols, width), left_high, left_low, high, low)
 
 
 def local(matrix):
     row_count = lax.axis_size("row")
     col_count = lax.axis_size("col")
-    row_index = lax.axis_index("row")
-    col_index = lax.axis_index("col")
     cyc_rows, width, cyc_cols, _ = matrix.shape
     n_rows, n_cols = cyc_rows * width, cyc_cols * width
-    lanes = jnp.arange(width, dtype=jnp.int32)
-    glob_rows = (
-        (jnp.arange(cyc_rows, dtype=jnp.int32)[:, None] * row_count + row_index) * width + lanes
-    ).reshape(-1)
-    glob_cols = (
-        (jnp.arange(cyc_cols, dtype=jnp.int32)[:, None] * col_count + col_index) * width + lanes
-    ).reshape(-1)
-
-    def columns_of(strip):
-        return jnp.transpose(strip, (1, 2, 0)).reshape(n_cols, width)
-
-    raw_rows = carry_rows(matrix, col_count)
-    strip = spread_strip(matrix, 0, 0, 0)
-
-    w_rows, w_cols, z_rows, z_cols = [], [], [], []
-    w_next, z_next = [], []
-    for k in range(PANELS):
-        first = (k + 1) * width
-        cols, rows = columns_of(strip), raw_rows[k]
-        if k:
-            inner = jnp.concatenate([w_next[0], z_next[0]], axis=1).T
-            cols = cols - dot_highest(jnp.concatenate([z_cols[0], w_cols[0]], axis=1), inner)
-            rows = rows - dot_highest(jnp.concatenate([z_rows[0], w_rows[0]], axis=1), inner)
-        cols = jnp.where((glob_cols >= first)[:, None], cols, 0.0)
-        rows = jnp.where((glob_rows >= first)[:, None], rows, 0.0)
-        top_at = ((k + 1) // col_count) * width
-        holds_top = col_index == (k + 1) % col_count
-        top_part = jnp.where(holds_top, cols[top_at : top_at + width], 0.0)
-        both = total(jnp.concatenate([dot_highest(cols.T, cols), top_part], axis=0), 1)
-        inv_lower, w_top = factorize(both)
-        unit_rows = (glob_rows[:, None] - first == lanes[None, :]).astype(jnp.float32)
-        wr = dot_highest(rows, inv_lower.T) - unit_rows
-        old = None
-        if k:
-            old = (
-                jnp.concatenate([w_cols[0], z_cols[0]], axis=1),
-                jnp.concatenate([z_rows[0], w_rows[0]], axis=1),
-            )
-        strip_of = ((k + 1) % row_count, (k + 1) // row_count) if k + 1 < PANELS else None
-        wc, inverse, y_rows, y_cols, *rest = panel_product(
-            matrix, cols, inv_lower, w_top, k + 1, old, strip_of, 2 + k
-        )
-        strip = rest[0] if rest else None
-        y_rows = y_rows.reshape(n_rows, width)
-        y_cols = y_cols.reshape(n_cols, width)
-        next_part = jnp.where(holds_top, y_cols[top_at : top_at + width], 0.0)
-        both = total(jnp.concatenate([dot_highest(wc.T, y_cols), next_part], axis=0), 1)
-        middle, y_next = both[:width], both[width:]
-        core = 0.5 * dot_highest(dot_highest(inverse, middle), inverse.T)
-        finish = jnp.concatenate([inverse.T, -core], axis=0)
-        w_rows.append(wr)
-        w_cols.append(wc)
-        w_next.append(w_top)
-        z_rows.append(dot_highest(jnp.concatenate([y_rows, wr], axis=1), finish))
-        z_cols.append(dot_highest(jnp.concatenate([y_cols, wc], axis=1), finish))
-        z_next.append(dot_highest(jnp.concatenate([y_next, w_top], axis=1), finish))
-
-    left = jnp.concatenate([x for k in range(PANELS) for x in (z_rows[k], w_rows[k])], axis=1)
-    right = jnp.concatenate([x for k in range(PANELS) for x in (w_cols[k], z_cols[k])], axis=1)
-    reduced = apply_update(matrix, left, right).reshape(matrix.shape)
-    bases = jnp.concatenate(w_rows, axis=1).reshape(cyc_rows, width, PANELS * width)
+
+    strip, raw = spread(matrix, 0, 0, 0, 0, 0)
+    cols, own, lower, w_top, raw = prepare(
+        strip, raw, 1, None, matrix, (1 % col_count, 1 // col_count), 1
+    )
+    strip_of = (1 % row_count, 1 // row_count)
+    wc, inverse, y_rows, y_cols, wr, both, strip = panel_product(
+        matrix, cols, lower, w_top, own, 1, None, strip_of, 2
+    )
+    later = [
+        both,
+        inverse,
+        w_top,
+        y_cols.reshape(n_cols, width),
+        wc,
+        y_rows.reshape(n_rows, width),
+        wr,
+    ]
+    cols, own, lower, w_top, old_cols, old_rows = prepare(strip, raw, 2, later, matrix, None, 3)
+    wc, inverse, y_rows, y_cols, wr_last, both = panel_product(
+        matrix, cols, lower, w_top, own, 2, (old_cols, old_rows), None, 4
+    )
+    y_rows, y_cols = y_rows.reshape(n_rows, width), y_cols.reshape(n_cols, width)
+    factors = finish_factors(both, inverse, y_cols, wc, y_rows, wr_last, old_cols, old_rows)
+    reduced = apply_update(matrix, *factors).reshape(matrix.shape)
+    bases = jnp.concatenate([wr, wr_last], axis=1).reshape(cyc_rows, width, PANELS * width)
     return (reduced, bases)
 
 

time: 419 us -> 330 us (0.79); the launches traced: 412 us -> 330 us
  matrix products: 51.2 us -> 0 us
  other arithmetic: 25.5 us -> 1.46 us
  Pallas kernels: 305 us -> 327 us
  local copies, waits for them, and re-layouts: 19.1 us -> 0.01 us
  starting transfers between devices: 9.6 us -> 0 us
    dot_general x17 -> x0, matrix products: 51.2 us -> none  [dot_highest(): jnp.dot(left, right, precision=lax.Precision.HIGHEST, preferred_element_t...]
    pallas_call x7 -> x4, Pallas kernels: 116 us -> 128 us  [the longest x2 83.1 us: prepare(): pl.pallas_call(functools.partial(prepare_kernel, first, later is not None...]
    pallas_call x2, Pallas kernels: 148 us -> 159 us  [panel_product(): pl.pallas_call(functools.partial(panel_kernel, first, min(8, cyc_cols), m...]
    concatenate x7 -> x1, other arithmetic: 11.5 us -> 1.46 us  [local(): jnp.concatenate([wr, wr_last], axis=1)]
    ppermute x3 -> x0, starting transfers between devices: 9.6 us -> none  [carry_rows(): moving = lax.ppermute(moving, 'col', pairs)]
    select_n x7 -> x0, other arithmetic: 9.46 us -> none  [the longest x2 5.44 us: local(): cols = jnp.where((glob_cols >= first)[:, None], cols, 0.0)]
    slice x3 -> x0, local copies, waits for them, and re-layouts: 5.77 us -> none  [the longest x1 4.04 us: carry_rows(): own = matrix[:, :, 0, :].reshape(-1, matrix.shape[3])]
    transpose x2 -> x0, local copies, waits for them, and re-layouts: 4.83 us -> none  [columns_of(): return jnp.transpose(strip, (1, 2, 0)).reshape(n_cols, width)]
  transfers between devices with their start and end apart: 3 -> 0, of which waited for: 0 -> 0; matrix products, arithmetic and copies ran while one was open for 12% -> 0% of each run, Pallas kernels for 41% -> 0%
where the time goes in v1:
time: 330 us
  Pallas kernels  327 us (99%)
    pallas_call x2, Pallas kernels, panel_product(): pl.pallas_call(functools.partial(panel_kernel, first, min(8, cyc_cols), m...  159 us
    pallas_call x2, Pallas kernels, prepare(): pl.pallas_call(functools.partial(prepare_kernel, first, later is not None...  83.1 us
    pallas_call x1, Pallas kernels, apply_update(): pl.pallas_call(functools.partial(update_kernel, min(4, cyc_cols)), grid=(...  40.3 us
    pallas_call x1, Pallas kernels, spread(): pl.pallas_call(functools.partial(spread_kernel, root, layer, col_root, co...  30.8 us
    pallas_call x1, Pallas kernels, finish_factors(): pl.pallas_call(finish_kernel, out_shape=[left, left, right, right], compi...  14.4 us

profile of v1, /device:TPU:0, one launch (start us, length us, event | category | flops | bytes accessed | tf_op | source)
XLA Modules:
  0.0 329.6 jit_solution(4118026832124203477)
XLA Ops:
  0.6 30.8 %shard_map.30 = (f32[128,32,128]{2,1,0:T(8,128)}, f32[16,128,128]{2,1,0:T(8,128)}) custom-call(f32[16,128,32,128]{3,2,1,0:T(8,128)} %refs_5_.1), custom_call_target="tpu_custom_call" | custom-call | tf_op jit(solution)/shard_map/pallas_call | solution.py:260
  31.5 53.1 %shard_map.31 = (f32[4096,128]{1,0:T(8,128)}, f32[2048,128]{1,0:T(8,128)}, f32[128,128]{1,0:T(8,128)}, f32[128,128]{1,0:T(8,128)}, f32[16,128,128]{2,1,0:T(8,128)}) custom-call(f32[128,32,128]{2,1,0:T(8,128)} %get-tuple-element.32.refs_0_, f32[16,128,128]{2,1,0:T(8,128)} %get-tuple-element.33.refs_1_, f32[16,128,32,128]{3,2,1,0:T(8,128)} %refs_5_.1), custom_call_target="tpu_custom_call" | custom-call | tf_op jit(solution)/shard_map/pallas_call | solution.py:610
  84.6 82.3 %shard_map.32 = (f32[4096,128]{1,0:T(8,128)}, f32[128,128]{1,0:T(8,128)}, f32[4,2,256,128]{3,2,1,0:T(8,128)}, f32[16,2,128,128]{3,2,1,0:T(8,128)}, f32[2048,128]...) custom-call(f32[2048,32,128]{2,1,0:T(8,128)} %bitcast.7, f32[4096,128]{1,0:T(8,128)} %get-tuple-element.34.refs_1_, ...), custom_call_target="tpu_custom_call" | custom-call | tf_op jit(solution)/shard_map/pallas_call | solution.py:957
  166.9 30.0 %shard_map.33 = (f32[4096,128]{1,0:T(8,128)}, f32[2048,128]{1,0:T(8,128)}, f32[128,128]{1,0:T(8,128)}, f32[128,128]{1,0:T(8,128)}, f32[4096,256]{1,0:T(8,128)}, /*index=5*/f32[2048,256]{1,0:T(8,128)}) custom-call(f32[128,32,128]{2,1,0:T(8,128)} %get-tuple-element.38.refs_0_, f32[16,128,128]{2,1,0:T(8,128)} %get-tuple-element.39.refs_1_, ...), custom_call_target="tpu_custom_call" | custom-call | tf_op jit(solution)/shard_map/pallas_call | solution.py:610
  196.9 76.3 %shard_map.34 = (f32[4096,128]{1,0:T(8,128)}, f32[128,128]{1,0:T(8,128)}, f32[4,2,256,128]{3,2,1,0:T(8,128)}, f32[16,2,128,128]{3,2,1,0:T(8,128)}, f32[2048,128]{1,0:T(8,128)}, /*index=5*/f32[8,32,128]{2,1,0:T(8,128)}) custom-call(f32[2048,32,128]{2,1,0:T(8,128)} %bitcast.8, f32[4096,128]{1,0:T(8,128)} %get-tuple-element.46.refs_1_, ...), custom_call_target="tpu_custom_call" | custom-call | tf_op jit(solution)/shard_map/pallas_call | solution.py:957
  273.3 0.0 copy-start
  273.3 0.0 copy-start.1
  273.3 14.4 %shard_map.35 = (bf16[2048,512]{1,0:T(8,128)(2,1)}, bf16[2048,512]{1,0:T(8,128)(2,1)}, bf16[512,4096]{1,0:T(8,128)(2,1)}, bf16[512,4096]{1,0:T(8,128)(2,1)}) custom-call(f32[8,32,128]{2,1,0:T(8,128)} %get-tuple-element.52.both_ref, f32[128,128]{1,0:T(8,128)} %get-tuple-element.53.inverse_ref, f32[4096,128]{1,0:T(8,128)} %bitcast.12, ...), custom_call_target="tpu_custom_call" | custom-call | tf_op jit(solution)/shard_map/pallas_call | solution.py:1055
  287.6 0.0 copy-done
  287.7 0.0 copy-done.1
  287.7 1.5 pad_maximum_fusion
  289.1 40.3 %shard_map.36 = f32[2048,32,128]{2,1,0:T(8,128)} custom-call(f32[2048,32,128]{2,1,0:T(8,128)} %bitcast.9, bf16[2048,512]{1,0:T(8,128)(2,1)} %get-tuple-element.58.uh_ref, bf16[2048,512]{1,0:T(8,128)(2,1)} %get-tuple-element.59.ul_ref, bf16[512,4096]{1,0:T(8,128)(2,1)} %get-tuple-element.60.vh_ref, bf16[512,4096]{1,0:T(8,128)(2,1)} %get-tuple-element.61.vl_ref), custom_call_target="tpu_custom_call" | custom-call | tf_op jit(solution)/shard_map/pallas_call | solution.py:1070
Async XLA Ops:
  273.3 14.4 %copy-start = (f32[2048,128]{1,0:T(8,128)S(1)}, f32[2048,128]{1,0:T(8,128)}, u32[]{:S(2)}) copy-start(f32[2048,128]{1,0:T(8,128)} %get-tuple-element.45.refs_8_) | copy-start | bytes 3145732
  273.3 14.4 %copy-start.1 = (f32[2048,128]{1,0:T(8,128)S(1)}, f32[2048,128]{1,0:T(8,128)}, u32[]{:S(2)}) copy-start(f32[2048,128]{1,0:T(8,128)} %get-tuple-element.57.w_rows_ref) | copy-start | bytes 3145732

commit v2 on v1

--- a/solution.py
+++ b/solution.py
@@ -195,23 +195,21 @@
         def _():
             for i in range(self.count):
                 self.local(i).start()
-            for i in range(self.count):
-                self.local(i).wait()
-                for side in range(2):
-
-                    @pl.when(self.ways[side])
-                    def _():
-                        self.onward(i, side).start()
 
     def serve(self, i):
+        @pl.when(self.col == self.root)
+        def _():
+            self.local(i).wait()
+
         @pl.when(self.col != self.root)
         def _():
             self.onward(i, 0).wait_recv()
-            for side in range(2):
-
-                @pl.when(self.ways[side])
-                def _():
-                    self.onward(i, side).start()
+
+        for side in range(2):
+
+            @pl.when(self.ways[side])
+            def _():
+                self.onward(i, side).start()
 
     def serve_turn(self, turn):
         far = jnp.maximum(self.col - self.root, self.root - self.col)
@@ -967,13 +965,54 @@
 
 
 def update_kernel(
-    group, a_ref, uh_ref, ul_ref, vh_ref, vl_ref, out_ref, held, done, sems, out_sems
+    group,
+    a_ref,
+    both_ref,
+    inverse_ref,
+    y_cols_ref,
+    w_cols_ref,
+    old_cols_ref,
+    y_rows_ref,
+    w_rows_ref,
+    old_rows_ref,
+    out_ref,
+    held,
+    done,
+    vh_ref,
+    vl_ref,
+    finish_ref,
+    sems,
+    out_sems,
 ):
-    tile = uh_ref.shape[0]
+    tile = w_rows_ref.shape[0]
     cyc_cols, width = a_ref.shape[1:]
     step, steps = pl.program_id(0), pl.num_programs(0)
     slot, copies = fetch_tiles(a_ref, held, sems, tile)
-    high, low = uh_ref[...], ul_ref[...]
+
+    @pl.when(step == 0)
+    def _():
+        inverse = inverse_ref[...]
+        core = 0.5 * transposed_dot(dot_highest(inverse, get_half(both_ref, 0)), inverse)
+        finish_ref[...] = side_by_side(jnp.concatenate([inverse.T, -core], axis=0))
+        rows = min(4, cyc_cols) * width
+
+        @pl.loop(0, cyc_cols * width // rows)
+        def _(chunk):
+            where = pl.ds(pl.multiple_of(chunk * rows, rows), rows)
+            w = w_cols_ref[where, :]
+            z = three_term(
+                split(jnp.concatenate([y_cols_ref[where, :], w], axis=1)), finish_ref[...], dot_f32
+            )
+            for at, value in ((0, old_cols_ref[where, :]), (2 * width, w), (3 * width, z)):
+                v_high, v_low = split(value.T)
+                vh_ref[at : at + value.shape[1], where] = v_high
+                vl_ref[at : at + value.shape[1], where] = v_low
+
+    w = w_rows_ref[...]
+    z = three_term(
+        split(jnp.concatenate([y_rows_ref[...], w], axis=1)), finish_ref[...], dot_f32
+    )
+    high, low = split(jnp.concatenate([old_rows_ref[...], z, w], axis=1))
 
     def stores(index, where):
         return [
@@ -1013,69 +1052,40 @@
                 copy.wait()
 
 
-def finish_kernel(
-    both_ref, inverse_ref, y_cols_ref, w_cols_ref, y_rows_ref, w_rows_ref,
-    old_cols_ref, old_rows_ref, lh_ref, ll_ref, rh_ref, rl_ref,
-):
-    width = inverse_ref.shape[0]
-    inverse = inverse_ref[...]
-    core = 0.5 * transposed_dot(dot_highest(inverse, get_half(both_ref, 0)), inverse)
-    finish = side_by_side(jnp.concatenate([inverse.T, -core], axis=0))
-    step = 4 * width
-
-    @pl.loop(0, y_rows_ref.shape[0] // step)
-    def _(group):
-        where = pl.ds(pl.multiple_of(group * step, step), step)
-        w = w_rows_ref[where, :]
-        z = three_term(
-            split(jnp.concatenate([y_rows_ref[where, :], w], axis=1)), finish, dot_f32
-        )
-        for at, value in ((0, old_rows_ref[where, :]), (2 * width, z), (3 * width, w)):
-            high, low = split(value)
-            lh_ref[where, at : at + value.shape[1]] = high
-            ll_ref[where, at : at + value.shape[1]] = low
-
-    @pl.loop(0, y_cols_ref.shape[0] // step)
-    def _(group):
-        where = pl.ds(pl.multiple_of(group * step, step), step)
-        w = w_cols_ref[where, :]
-        z = three_term(
-            split(jnp.concatenate([y_cols_ref[where, :], w], axis=1)), finish, dot_f32
-        )
-        for at, value in ((0, old_cols_ref[where, :]), (2 * width, w), (3 * width, z)):
-            high, low = split(value.T)
-            rh_ref[at : at + value.shape[1], where] = high
-            rl_ref[at : at + value.shape[1], where] = low
-
-
-def finish_factors(both, inverse, y_cols, w_cols, y_rows, w_rows, old_cols, old_rows):
-    width = inverse.shape[0]
-    left = jax.ShapeDtypeStruct((y_rows.shape[0], 4 * width), jnp.bfloat16)
-    right = jax.ShapeDtypeStruct((4 * width, y_cols.shape[0]), jnp.bfloat16)
-    return pl.pallas_call(
-        finish_kernel,
-        out_shape=[left, left, right, right],
-        compiler_params=pltpu.CompilerParams(vmem_limit_bytes=VMEM_LIMIT),
-    )(both, inverse, y_cols, w_cols, y_rows, w_rows, old_cols, old_rows)
-
-
-def apply_update(matrix, left_high, left_low, high, low):
+def apply_update(matrix, both, inverse, y_cols, w_cols, old_cols, y_rows, w_rows, old_rows):
     cyc_rows, width, cyc_cols, _ = matrix.shape
-    n_rows, depth = left_high.shape
+    n_rows = cyc_rows * width
     tile = min(256, n_rows)
-    whole = pl.BlockSpec(high.shape, lambda i: (0, 0), pipeline_mode=pl.Buffered(1))
-    some = pl.BlockSpec((tile, depth), lambda i: (i, 0))
+
+    def whole(x):
+        return pl.BlockSpec(x.shape, lambda i: (0,) * x.ndim, pipeline_mode=pl.Buffered(1))
+
+    def some(x):
+        return pl.BlockSpec((tile, x.shape[1]), lambda i: (i, 0))
+
     held = pltpu.VMEM((2, cyc_cols, tile, width), jnp.float32)
+    right = pltpu.VMEM((4 * width, cyc_cols * width), jnp.bfloat16)
     sems = pltpu.SemaphoreType.DMA((2, cyc_cols))
+    fixed, moving = [both, inverse, y_cols, w_cols, old_cols], [y_rows, w_rows, old_rows]
     return pl.pallas_call(
         functools.partial(update_kernel, min(4, cyc_cols)),
         grid=(n_rows // tile,),
         out_shape=jax.ShapeDtypeStruct((n_rows, cyc_cols, width), jnp.float32),
-        in_specs=[pl.BlockSpec(memory_space=pl.ANY), some, some, whole, whole],
+        in_specs=[pl.BlockSpec(memory_space=pl.ANY)]
+        + [whole(x) for x in fixed]
+        + [some(x) for x in moving],
         out_specs=pl.BlockSpec(memory_space=pl.ANY),
-        scratch_shapes=[held, held, sems, sems],
+        scratch_shapes=[
+            held,
+            held,
+            right,
+            right,
+            pltpu.VMEM((2 * width, 2 * width), jnp.bfloat16),
+            sems,
+            sems,
+        ],
         compiler_params=pltpu.CompilerParams(vmem_limit_bytes=VMEM_LIMIT),
-    )(matrix.reshape(n_rows, cyc_cols, width), left_high, left_low, high, low)
+    )(matrix.reshape(n_rows, cyc_cols, width), *fixed, *moving)
 
 
 def local(matrix):
@@ -1106,8 +1116,9 @@
         matrix, cols, lower, w_top, own, 2, (old_cols, old_rows), None, 4
     )
     y_rows, y_cols = y_rows.reshape(n_rows, width), y_cols.reshape(n_cols, width)
-    factors = finish_factors(both, inverse, y_cols, wc, y_rows, wr_last, old_cols, old_rows)
-    reduced = apply_update(matrix, *factors).reshape(matrix.shape)
+    reduced = apply_update(
+        matrix, both, inverse, y_cols, wc, old_cols, y_rows, wr_last, old_rows
+    ).reshape(matrix.shape)
     bases = jnp.concatenate([wr, wr_last], axis=1).reshape(cyc_rows, width, PANELS * width)
     return (reduced, bases)
 

time: 330 us -> 312 us (0.945)
  Pallas kernels: 327 us -> 309 us
    pallas_call x1 -> x0, Pallas kernels: 14.4 us -> none  [finish_factors(): pl.pallas_call(finish_kernel, out_shape=[left, left, right, right], compi...]
    pallas_call x2, Pallas kernels: 159 us -> 154 us  [panel_product(): pl.pallas_call(functools.partial(panel_kernel, first, min(8, cyc_cols), m...]
where the time goes in v2:
time: 312 us
  Pallas kernels  309 us (99%)
    pallas_call x2, Pallas kernels, panel_product(): pl.pallas_call(functools.partial(panel_kernel, first, min(8, cyc_cols), m...  154 us
    pallas_call x2, Pallas kernels, prepare(): pl.pallas_call(functools.partial(prepare_kernel, first, later is not None...  81.7 us
    pallas_call x1, Pallas kernels, apply_update(): pl.pallas_call(functools.partial(update_kernel, min(4, cyc_cols)), grid=(...  43.3 us
    pallas_call x1, Pallas kernels, spread(): pl.pallas_call(functools.partial(spread_kernel, root, layer, col_root, co...  30.8 us

profile of v2, /device:TPU:0, one launch (start us, length us, event | category | flops | bytes accessed | tf_op | source)
XLA Modules:
  0.0 311.5 jit_solution(7766419505393880918)
XLA Ops:
  0.6 30.8 %shard_map.30 = (f32[128,32,128]{2,1,0:T(8,128)}, f32[16,128,128]{2,1,0:T(8,128)}) custom-call(f32[16,128,32,128]{3,2,1,0:T(8,128)} %refs_5_.1), custom_call_target="tpu_custom_call" | custom-call | tf_op jit(solution)/shard_map/pallas_call | solution.py:258
  31.5 51.7 %shard_map.31 = (f32[4096,128]{1,0:T(8,128)}, f32[2048,128]{1,0:T(8,128)}, f32[128,128]{1,0:T(8,128)}, f32[128,128]{1,0:T(8,128)}, f32[16,128,128]{2,1,0:T(8,128)}) custom-call(f32[128,32,128]{2,1,0:T(8,128)} %get-tuple-element.28.refs_0_, f32[16,128,128]{2,1,0:T(8,128)} %get-tuple-element.29.refs_1_, f32[16,128,32,128]{3,2,1,0:T(8,128)} %refs_5_.1), custom_call_target="tpu_custom_call" | custom-call | tf_op jit(solution)/shard_map/pallas_call | solution.py:608
  83.2 77.2 %shard_map.32 = (f32[4096,128]{1,0:T(8,128)}, f32[128,128]{1,0:T(8,128)}, f32[4,2,256,128]{3,2,1,0:T(8,128)}, f32[16,2,128,128]{3,2,1,0:T(8,128)}, f32[2048,128]...) custom-call(f32[2048,32,128]{2,1,0:T(8,128)} %bitcast.7, f32[4096,128]{1,0:T(8,128)} %get-tuple-element.30.refs_1_, ...), custom_call_target="tpu_custom_call" | custom-call | tf_op jit(solution)/shard_map/pallas_call | solution.py:955
  160.3 30.0 %shard_map.33 = (f32[4096,128]{1,0:T(8,128)}, f32[2048,128]{1,0:T(8,128)}, f32[128,128]{1,0:T(8,128)}, f32[128,128]{1,0:T(8,128)}, f32[4096,256]{1,0:T(8,128)}, /*index=5*/f32[2048,256]{1,0:T(8,128)}) custom-call(f32[128,32,128]{2,1,0:T(8,128)} %get-tuple-element.34.refs_0_, f32[16,128,128]{2,1,0:T(8,128)} %get-tuple-element.35.refs_1_, ...), custom_call_target="tpu_custom_call" | custom-call | tf_op jit(solution)/shard_map/pallas_call | solution.py:608
  190.3 76.4 %shard_map.34 = (f32[4096,128]{1,0:T(8,128)}, f32[128,128]{1,0:T(8,128)}, f32[4,2,256,128]{3,2,1,0:T(8,128)}, f32[16,2,128,128]{3,2,1,0:T(8,128)}, f32[2048,128]{1,0:T(8,128)}, /*index=5*/f32[8,32,128]{2,1,0:T(8,128)}) custom-call(f32[2048,32,128]{2,1,0:T(8,128)} %bitcast.8, f32[4096,128]{1,0:T(8,128)} %get-tuple-element.42.refs_1_, ...), custom_call_target="tpu_custom_call" | custom-call | tf_op jit(solution)/shard_map/pallas_call | solution.py:955
  266.7 0.0 copy-start
  266.7 0.0 copy-start.1
  266.7 43.3 %shard_map.35 = f32[2048,32,128]{2,1,0:T(8,128)} custom-call(f32[2048,32,128]{2,1,0:T(8,128)} %bitcast.9, f32[8,32,128]{2,1,0:T(8,128)} %get-tuple-element.48.both_ref, f32[128,128]{1,0:T(8,128)} %get-tuple-element.49.inverse_ref, f32[4096,128]{1,0:T(8,128)} %bitcast.12, f32[4096,128]{1,0:T(8,128)} %get-tuple-element.51.w_cols_ref, ...), custom_call_target="tpu_custom_call" | custom-call | tf_op jit(solution)/shard_map/pallas_call | solution.py:1070
  310.0 0.0 copy-done
  310.1 0.0 copy-done.1
  310.1 1.5 pad_maximum_fusion
Async XLA Ops:
  266.7 43.4 %copy-start = (f32[2048,128]{1,0:T(8,128)S(1)}, f32[2048,128]{1,0:T(8,128)}, u32[]{:S(2)}) copy-start(f32[2048,128]{1,0:T(8,128)} %get-tuple-element.53.w_rows_ref) | copy-start | bytes 3145732
  266.7 43.4 %copy-start.1 = (f32[2048,128]{1,0:T(8,128)S(1)}, f32[2048,128]{1,0:T(8,128)}, u32[]{:S(2)}) copy-start(f32[2048,128]{1,0:T(8,128)} %get-tuple-element.41.refs_8_) | copy-start | bytes 3145732

commit v3 on v2

--- a/solution.py
+++ b/solution.py
@@ -652,8 +652,9 @@
             for c in range(cyc_cols)
         ]
 
-    for copy in fetch(0, 0):
-        copy.start()
+    for ahead in range(2):
+        for copy in fetch(ahead, ahead):
+            copy.start()
     strip = None
     if root_strip is not None:
         root, layer = root_strip
@@ -700,12 +701,6 @@
     @pl.loop(0, tiles)
     def _(index):
         slot = lax.rem(index, 2)
-
-        @pl.when(index + 1 < tiles)
-        def _():
-            for copy in fetch(index + 1, 1 - slot):
-                copy.start()
-
         for copy in fetch(index, slot):
             copy.wait()
         total = None
@@ -721,6 +716,11 @@
             old = split(old_rows_ref[pl.ds(start, tile), :])
             total = total - three_term(old, old_weights[...], dot_f32)
         part[q, piece] = total
+
+        @pl.when(index + 2 < tiles)
+        def _():
+            for copy in fetch(index + 2, slot):
+                copy.start()
 
         @pl.when(index < tiles - pieces)
         def _():

time: 312 us -> 311 us (level)
  no operation moved by 1% of the time
where the time goes in v3:
time: 311 us
  Pallas kernels  309 us (99%)
    pallas_call x2, Pallas kernels, panel_product(): pl.pallas_call(functools.partial(panel_kernel, first, min(8, cyc_cols), m...  153 us
    pallas_call x2, Pallas kernels, prepare(): pl.pallas_call(functools.partial(prepare_kernel, first, later is not None...  81.6 us
    pallas_call x1, Pallas kernels, apply_update(): pl.pallas_call(functools.partial(update_kernel, min(4, cyc_cols)), grid=(...  43.3 us
    pallas_call x1, Pallas kernels, spread(): pl.pallas_call(functools.partial(spread_kernel, root, layer, col_root, co...  30.8 us

profile of v3, /device:TPU:0, one launch (start us, length us, event | category | flops | bytes accessed | tf_op | source)
XLA Modules:
  0.0 311.1 jit_solution(406147437845076819)
XLA Ops:
  0.6 30.8 %shard_map.30 = (f32[128,32,128]{2,1,0:T(8,128)}, f32[16,128,128]{2,1,0:T(8,128)}) custom-call(f32[16,128,32,128]{3,2,1,0:T(8,128)} %refs_5_.1), custom_call_target="tpu_custom_call" | custom-call | tf_op jit(solution)/shard_map/pallas_call | solution.py:258
  31.5 51.7 %shard_map.31 = (f32[4096,128]{1,0:T(8,128)}, f32[2048,128]{1,0:T(8,128)}, f32[128,128]{1,0:T(8,128)}, f32[128,128]{1,0:T(8,128)}, f32[16,128,128]{2,1,0:T(8,128)}) custom-call(f32[128,32,128]{2,1,0:T(8,128)} %get-tuple-element.28.refs_0_, f32[16,128,128]{2,1,0:T(8,128)} %get-tuple-element.29.refs_1_, f32[16,128,32,128]{3,2,1,0:T(8,128)} %refs_5_.1), custom_call_target="tpu_custom_call" | custom-call | tf_op jit(solution)/shard_map/pallas_call | solution.py:608
  83.2 77.3 %shard_map.32 = (f32[4096,128]{1,0:T(8,128)}, f32[128,128]{1,0:T(8,128)}, f32[4,2,256,128]{3,2,1,0:T(8,128)}, f32[16,2,128,128]{3,2,1,0:T(8,128)}, f32[2048,128]...) custom-call(f32[2048,32,128]{2,1,0:T(8,128)} %bitcast.7, f32[4096,128]{1,0:T(8,128)} %get-tuple-element.30.refs_1_, ...), custom_call_target="tpu_custom_call" | custom-call | tf_op jit(solution)/shard_map/pallas_call | solution.py:955
  160.5 29.9 %shard_map.33 = (f32[4096,128]{1,0:T(8,128)}, f32[2048,128]{1,0:T(8,128)}, f32[128,128]{1,0:T(8,128)}, f32[128,128]{1,0:T(8,128)}, f32[4096,256]{1,0:T(8,128)}, /*index=5*/f32[2048,256]{1,0:T(8,128)}) custom-call(f32[128,32,128]{2,1,0:T(8,128)} %get-tuple-element.34.refs_0_, f32[16,128,128]{2,1,0:T(8,128)} %get-tuple-element.35.refs_1_, ...), custom_call_target="tpu_custom_call" | custom-call | tf_op jit(solution)/shard_map/pallas_call | solution.py:608
  190.4 75.8 %shard_map.34 = (f32[4096,128]{1,0:T(8,128)}, f32[128,128]{1,0:T(8,128)}, f32[4,2,256,128]{3,2,1,0:T(8,128)}, f32[16,2,128,128]{3,2,1,0:T(8,128)}, f32[2048,128]{1,0:T(8,128)}, /*index=5*/f32[8,32,128]{2,1,0:T(8,128)}) custom-call(f32[2048,32,128]{2,1,0:T(8,128)} %bitcast.8, f32[4096,128]{1,0:T(8,128)} %get-tuple-element.42.refs_1_, ...), custom_call_target="tpu_custom_call" | custom-call | tf_op jit(solution)/shard_map/pallas_call | solution.py:955
  266.3 0.0 copy-start
  266.3 0.0 copy-start.1
  266.3 43.3 %shard_map.35 = f32[2048,32,128]{2,1,0:T(8,128)} custom-call(f32[2048,32,128]{2,1,0:T(8,128)} %bitcast.9, f32[8,32,128]{2,1,0:T(8,128)} %get-tuple-element.48.both_ref, f32[128,128]{1,0:T(8,128)} %get-tuple-element.49.inverse_ref, f32[4096,128]{1,0:T(8,128)} %bitcast.12, f32[4096,128]{1,0:T(8,128)} %get-tuple-element.51.w_cols_ref, ...), custom_call_target="tpu_custom_call" | custom-call | tf_op jit(solution)/shard_map/pallas_call | solution.py:1070
  309.6 0.0 copy-done
  309.6 0.0 copy-done.1
  309.7 1.5 pad_maximum_fusion
Async XLA Ops:
  266.3 43.4 %copy-start = (f32[2048,128]{1,0:T(8,128)S(1)}, f32[2048,128]{1,0:T(8,128)}, u32[]{:S(2)}) copy-start(f32[2048,128]{1,0:T(8,128)} %get-tuple-element.53.w_rows_ref) | copy-start | bytes 3145732
  266.3 43.4 %copy-start.1 = (f32[2048,128]{1,0:T(8,128)S(1)}, f32[2048,128]{1,0:T(8,128)}, u32[]{:S(2)}) copy-start(f32[2048,128]{1,0:T(8,128)} %get-tuple-element.41.refs_8_) | copy-start | bytes 3145732
